TPU v7x, 256 devices: a whole 4x4x8 slice. The times are simulated.
256 devices in a mesh: cells: 64 (over x_lo, y, z), tracers: 4 (over x_hi, core).
Axes of the slice: x: 4 (x_hi: 2, x_lo: 2; x = x_hi * 2 + x_lo), y: 4, z: 8, core: 2. Of those that a mesh axis runs over, the one named last changes fastest.
Arguments:
- pulses: float32 [4096, 256, 128], P('tracers', 'cells'), may hold values from -6 to 6
- wind_x: float32 [256, 128], P('cells'), may hold values from -0.24 to 0.24
- wind_y: float32 [256, 128], P('cells'), may hold values from -0.24 to 0.24
- obs_tile: int32 [8192, 1], P('cells'), may hold values from 0 to 63; in each aligned block of 128 rows (0 to 127, 128 to 255, ...) at most 4 rows name the same one
- obs_weight: bfloat16 [8192, 512], P('cells'), may hold values from 0.099609375 to 10
- obs_precision: bfloat16 [8192], P('cells'), may hold values from 0.0029907227 to 0.099609375
Outputs:
- gram: float32 [4096, 4096], P('cells', 'tracers')
Inputs may be any that keep to these rules, and one draw needn't show every extreme that they name: `obs_tile`: among the rows of one index of cells no tile is named by more than 4 rows, a bound that some block reaches of them.
All inputs are finite; a program needn't handle non-finite values.
Results may differ from a plain program's by a relative error of at most 0.0031.
Values may be sent and summed in bfloat16 or wider, within the bound.
No kernel may reach another device: no remote copies, remote signals or barrier semaphores. Data moves between devices by JAX's collectives and lax.ppermute only.
A program may use at most 64 MiB of HBM per device.

v0:
```python
import functools

import jax
import jax.numpy as jnp
from jax import lax
from jax.experimental import pallas as pl
from jax.experimental.pallas import tpu as pltpu
from jax.sharding import Mesh, PartitionSpec as P


STEPS = 3
CHUNKS = 4
GRANT = 16 * 1024 * 1024
CAP = 4
XY = ("xl", "y")
CELLS = ("xl", "y", "z")
TRACERS = ("xh", "core")
PLANE = XY + TRACERS


def shifted(value, axis, steps):
    count = lax.axis_size(axis)
    return lax.ppermute(value, axis, [(i, (i + steps) % count) for i in range(count)])


def exchanged(value, axis):
    return lax.all_to_all(value, axis, split_axis=0, concat_axis=0, tiled=True)


def edge_rows(pulse_ref, wind_x_ref, wind_y_ref, *refs):
    out_refs, (fetched_ref, winds_ref, sems) = refs[:-3], refs[-3:]
    tracers = pulse_ref.shape[0] // 4
    size = tracers // CHUNKS
    copies = []
    for k in range(CHUNKS):
        part = pl.ds(4 * k * size, 4 * size)
        copies.append(
            pltpu.make_async_copy(pulse_ref.at[part], fetched_ref.at[part], sems.at[k])
        )
    for k, ref in enumerate((wind_x_ref, wind_y_ref)):
        copies.append(pltpu.make_async_copy(ref, winds_ref.at[k], sems.at[CHUNKS + k]))
    for copy in copies:
        copy.start()
    for k in range(CHUNKS):
        copies[k].wait()
        rows = [
            fetched_ref[pl.ds(4 * k * size + r, size, 4), :].astype(jnp.bfloat16) for r in range(4)
        ]
        for part, (start, length) in enumerate(spans(tracers)):
            at = k * size - start
            if 0 <= at < length:
                for edge in range(2):
                    for r in range(STEPS):
                        out_refs[2 * part + edge][r * length + at : r * length + at + size] = rows[
                            r + edge
                        ]
    copies[CHUNKS].wait()
    copies[CHUNKS + 1].wait()
    winds = jnp.concatenate([winds_ref[0], winds_ref[1]], axis=0)
    coarse = winds.astype(jnp.bfloat16).astype(jnp.float32)
    both = jnp.concatenate([coarse, winds - coarse], axis=0).astype(jnp.bfloat16)
    for ref in out_refs:
        ref[ref.shape[0] - 16 :] = both


def spans(tracers):
    cut = tracers * 3 // 4
    return [(0, cut), (cut, tracers - cut)]


def edges(pulses, wind_x, wind_y):
    tracers = pulses.shape[0] // 4
    shapes = []
    for start, size in spans(tracers):
        shapes += [jax.ShapeDtypeStruct((STEPS * size + 16, 128), jnp.bfloat16)] * 2
    winds = [pltpu.with_memory_space_constraint(w, pltpu.HBM) for w in (wind_x, wind_y)]
    return pl.pallas_call(
        edge_rows,
        in_specs=[pl.BlockSpec(memory_space=pltpu.HBM)] * 3,
        out_specs=[pl.BlockSpec(memory_space=pltpu.VMEM)] * len(shapes),
        out_shape=shapes,
        scratch_shapes=[
            pltpu.VMEM(pulses.shape, jnp.float32),
            pltpu.VMEM((2, *wind_x.shape), jnp.float32),
            pltpu.SemaphoreType.DMA((CHUNKS + 2,)),
        ],
        compiler_params=pltpu.CompilerParams(vmem_limit_bytes=GRANT),
        name="edges",
    )(pulses, *winds)


PIECE = 64


def transport_body(
    pulse_ref, a0, a1, a2, b0, b1, b2, a_winds, b_winds, wind_x_ref, wind_y_ref, *refs
):
    out_ref, coef_ref = refs[-2:]
    count = out_ref.shape[0]

    @pl.when(pl.program_id(0) == 0)
    def _():
        above = a_winds[...].astype(jnp.float32)
        below = b_winds[...].astype(jnp.float32)
        above = above[0:8] + above[8:16]
        below = below[0:8] + below[8:16]
        wind_x = jnp.concatenate([above[2:4], wind_x_ref[...], below[0:2]], axis=0)
        wind_y = jnp.concatenate([above[6:8], wind_y_ref[...], below[4:6]], axis=0)
        next_y = jnp.concatenate([above[7:8], wind_y_ref[...], below[4:7]], axis=0)
        gain_x, loss_x = jnp.maximum(wind_x, 0.0), jnp.minimum(wind_x, 0.0)
        gain_y, loss_y = jnp.maximum(wind_y, 0.0), jnp.minimum(wind_y, 0.0)
        keep = 1.0 + loss_x - pltpu.roll(gain_x, 127, 1) + loss_y - jnp.maximum(next_y, 0.0)
        parts = [
            keep, gain_x, -pltpu.roll(loss_x, 127, 1), gain_y, -jnp.minimum(next_y, 0.0)
        ]
        for k, part in enumerate(parts):
            for w in range(8):
                coef_ref[k * 8 + w] = jnp.broadcast_to(part[w : w + 1], (PIECE, 128))

    for piece in range(count // PIECE):
        at = piece * PIECE
        field = (
            [ref[at : at + PIECE].astype(jnp.float32) for ref in (a0, a1, a2)]
            + [pulse_ref[pl.ds(4 * at + r, PIECE, 4), :] for r in range(4)]
            + [ref[at : at + PIECE].astype(jnp.float32) for ref in (b0, b1, b2)]
        )
        for step in range(STEPS):
            new = []
            for i in range(len(field) - 2):
                w = step + i
                here = field[i + 1]
                new.append(
                    coef_ref[w] * here
                    + coef_ref[8 + w] * pltpu.roll(here, 1, 1)
                    + coef_ref[16 + w] * pltpu.roll(here, 127, 1)
                    + coef_ref[24 + w] * field[i]
                    + coef_ref[32 + w] * field[i + 2]
                )
            field = new
        for r in range(4):
            out_ref[at : at + PIECE, r * 128 : (r + 1) * 128] = field[r].astype(jnp.bfloat16)


def transport(pulses, above, below, wind_x, wind_y, span, into=None, block=256):
    tracers = pulses.shape[0] // 4
    start, size = span
    skip, steps = start // block, size // block
    halo = [
        pl.BlockSpec((block, 128), lambda i, r=r: (r * steps + i, 0)) for r in range(STEPS)
    ]
    last = [pl.BlockSpec((16, 128), lambda i: (STEPS * size // 16, 0))] * 2
    wind = pl.BlockSpec((4, 128), lambda i: (0, 0))
    operands = [pulses, *[above] * 3, *[below] * 3, above, below, wind_x, wind_y]
    specs = [pl.BlockSpec((4 * block, 128), lambda i: (skip + i, 0))] + halo + halo + last
    specs += [wind, wind]
    aliases = {}
    if into is not None:
        aliases = {len(operands): 0}
        operands.append(into)
        specs.append(pl.BlockSpec(memory_space=pl.ANY))
    return pl.pallas_call(
        transport_body,
        grid=(steps,),
        in_specs=specs,
        out_specs=pl.BlockSpec((block, 512), lambda i: (skip + i, 0)),
        out_shape=jax.ShapeDtypeStruct((tracers, 512), jnp.bfloat16),
        scratch_shapes=[
            pltpu.VMEM((40, PIECE, 128), jnp.float32),
        ],
        input_output_aliases=aliases,
        compiler_params=pltpu.CompilerParams(vmem_limit_bytes=GRANT),
        name="transport",
    )(*operands)


def jacobian_body(rows_ref, low_ref, high_ref, out_ref, full_ref):
    @pl.when(pl.program_id(0) == 0)
    def _():
        count, width = rows_ref.shape
        mine = rows_ref[...].astype(jnp.float32).reshape(count // 8, 8, width)
        swap = pltpu.roll(mine, 4, 1)
        top = lax.broadcasted_iota(jnp.int32, mine.shape, 1) < 4
        left = jnp.where(top, mine, swap).reshape(count, width)
        right = jnp.where(top, swap, mine).reshape(count, width)
        full_ref[:, :width] = left.astype(jnp.bfloat16)
        full_ref[:, width:] = right.astype(jnp.bfloat16)

    dims = (((1,), (1,)), ((), ()))
    full = full_ref[...]
    low = lax.dot_general(full, low_ref[...], dims, preferred_element_type=jnp.float32)
    high = lax.dot_general(full, high_ref[...], dims, preferred_element_type=jnp.float32)
    row = lax.broadcasted_iota(jnp.int32, low.shape, 0)
    out_ref[...] = jnp.where((row & 4) == 0, low, high).astype(jnp.bfloat16)


def jacobian(rows, sampled, block=256):
    tracers = sampled.shape[0]
    count, width = rows.shape
    steps = tracers // 2 // block
    return pl.pallas_call(
        jacobian_body,
        grid=(steps,),
        in_specs=[
            pl.BlockSpec((count, width), lambda i: (0, 0)),
            pl.BlockSpec((block, 512), lambda i: (i, 0)),
            pl.BlockSpec((block, 512), lambda i: (steps + i, 0)),
        ],
        out_specs=pl.BlockSpec((count, block), lambda i: (0, i)),
        out_shape=jax.ShapeDtypeStruct((count, tracers // 2), jnp.bfloat16),
        scratch_shapes=[pltpu.VMEM((count, 2 * width), jnp.bfloat16)],
        compiler_params=pltpu.CompilerParams(vmem_limit_bytes=GRANT),
        name="jacobian",
    )(rows, sampled, sampled)


def gram_body(apart, place_ref, *refs):
    pieces, cols, outs, scratch = refs[:4], refs[4:12], refs[12:-3], refs[-3:]
    rows_ref, cols_ref, sum_ref = scratch
    block = cols[0].shape[0]
    parts = []
    for ref in pieces:
        parts += [ref[s : s + block] for s in range(0, ref.shape[0], block)]
    for k, part in enumerate(parts):
        at = pl.multiple_of(place_ref[k] * block, block)
        rows_ref[:, pl.ds(at, block)] = part.T
    for k, ref in enumerate(cols):
        at = pl.multiple_of(place_ref[8 + k] * block, block)
        cols_ref[pl.ds(at, block), :] = ref[...]
    tile = lax.dot_general(
        rows_ref[...], cols_ref[...], (((1,), (0,)), ((), ())), preferred_element_type=jnp.float32
    )
    if not apart:
        outs[0][...] = tile.astype(jnp.bfloat16)
        return
    sum_ref[...] = tile
    deep = len(outs)
    size = tile.shape[0] // deep
    for d, out_ref in enumerate(outs):
        at = pl.multiple_of(((place_ref[16] + d) % deep) * size, size)
        out_ref[...] = sum_ref[pl.ds(at, size), :].astype(out_ref.dtype)


def gram_tile(place, pieces, cols, apart):
    obs, width = cols[0].shape
    rows = pieces[0].shape[1]
    if apart:
        size = (rows // apart, width)
        shapes = [jax.ShapeDtypeStruct(size, jnp.float32)]
        shapes += [jax.ShapeDtypeStruct(size, jnp.bfloat16)] * (apart - 1)
    else:
        shapes = [jax.ShapeDtypeStruct((rows, width), jnp.bfloat16)]
    whole = pl.BlockSpec(memory_space=pltpu.VMEM)
    return pl.pallas_call(
        functools.partial(gram_body, apart),
        in_specs=[pl.BlockSpec(memory_space=pltpu.SMEM)] + [whole] * (len(pieces) + len(cols)),
        out_specs=[whole] * len(shapes),
        out_shape=shapes,
        scratch_shapes=[
            pltpu.VMEM((rows, len(cols) * obs), jnp.bfloat16),
            pltpu.VMEM((len(cols) * obs, width), jnp.bfloat16),
            pltpu.VMEM((rows, width), jnp.float32),
        ],
        compiler_params=pltpu.CompilerParams(vmem_limit_bytes=GRANT),
        name="gram",
    )(place, *pieces, *cols)


def on_device(pulses, wind_x, wind_y, obs_tile, obs_weight, obs_precision):
    tracers = pulses.shape[0]
    cells = lax.axis_size(CELLS)
    obs = obs_tile.shape[0]
    half = tracers // 2
    pulses = pulses.reshape(tracers * 4, 128)

    pulses = pltpu.with_memory_space_constraint(pulses, pltpu.HBM)
    messages = edges(pulses, wind_x, wind_y)
    halos = []
    for k in range(2):
        halos.append((shifted(messages[2 * k + 1], CELLS, 1), shifted(messages[2 * k], CELLS, -1)))
    sampled = None
    for span, (above, below) in zip(spans(tracers), halos):
        sampled = transport(pulses, above, below, wind_x, wind_y, span, sampled)

    tile = obs_tile[:, 0]
    order = jnp.arange(obs)
    earlier = (tile[:, None] == tile[None, :]) & (order[None, :] < order[:, None])
    slot = 2 * CAP * tile + jnp.sum(earlier.astype(jnp.int32), axis=1)
    lanes = jnp.arange(2 * CAP * cells)[None, :]
    chosen = [(slot[:, None] + CAP * h == lanes).astype(jnp.bfloat16) for h in range(2)]
    wide = obs_weight.astype(jnp.float32)
    averaging = (wide / jnp.sum(wide, axis=1, keepdims=True)).astype(jnp.bfloat16)
    split = obs_weight.shape[1] // 2
    rows_out = lax.dot_general(
        jnp.concatenate(chosen, axis=0),
        jnp.concatenate([averaging[:, :split], averaging[:, split:]], axis=0),
        (((0,), (0,)), ((), ())),
        preferred_element_type=jnp.float32,
    ).astype(jnp.bfloat16)
    rows_in = exchanged(rows_out.reshape(cells, 2 * CAP, split), CELLS)

    jac_tile = jacobian(rows_in.reshape(cells * 2 * CAP, split), sampled)
    group = lax.axis_size(XY)
    peers = lax.axis_size(TRACERS)
    deep = lax.axis_size("y")
    here = lax.axis_index(XY)
    odd = here % 2
    xl, y = lax.axis_index("xl"), lax.axis_index("y")
    owners = [here, (1 - xl) * deep + y]
    owners += [xl * deep + (y - d) % deep for d in range(1, deep)]
    owners += [(1 - xl) * deep + (y - d) % deep for d in range(1, deep)]
    tracer = lax.axis_index(TRACERS)
    row_owners = [2 * (tracer ^ flip) + (odd ^ s) for flip in (0, 2, 1, 3) for s in (0, 1)]
    place = jnp.stack(row_owners + owners + [lax.axis_index("z")]).astype(jnp.int32)
    precision = obs_precision.astype(jnp.float32)[:, None]
    even = odd == 0
    jac_tile, precision, place, even = lax.optimization_barrier((jac_tile, precision, place, even))
    jac_back = exchanged(jac_tile.reshape(cells, 2 * CAP, half), CELLS)
    jac_back = jac_back.reshape(cells * 2 * CAP, half)
    jac = [
        lax.dot_general(
            c, jac_back, (((1,), (0,)), ((), ())), preferred_element_type=jnp.float32
        )
        for c in chosen
    ]
    weighted = jnp.concatenate([(precision * j).astype(jnp.bfloat16) for j in jac], axis=1)
    cut = tracers * 5 // 8
    weighted = [weighted[:, :cut], weighted[:, cut:]]
    low, high = [j.astype(jnp.bfloat16) for j in jac]

    pairs = [(i // peers, i % peers) for i in range(group * peers)]
    to_same = [(a * peers + q, (2 * q + a % 2) * peers + a // 2) for a, q in pairs]
    to_cross = [(a * peers + q, (2 * q + 1 - a % 2) * peers + a // 2) for a, q in pairs]
    same = lax.ppermute(jnp.where(even, low, high), PLANE, to_same)
    cross = lax.ppermute(jnp.where(even, high, low), PLANE, to_cross)
    own = jnp.concatenate([same, cross], axis=0)
    across = shifted(own, "xh", 1)
    other = [shifted(own, "core", 1)]
    other.append(shifted(across, "core", 1))

    cols = []
    for part, value in enumerate(weighted):
        beside = shifted(value, "xl", 1)
        cols.append([value, beside])
        for source in (value, beside):
            for d in range(1, deep):
                cols[part].append(shifted(source, "y", d))

    depth = lax.axis_size("z")
    tile = gram_tile(place, [own, across, *other], cols[0], 0)[0]
    parts = exchanged(tile.reshape(depth, half // depth, cut), "z")
    total = jnp.sum(parts.astype(jnp.float32), axis=0)
    blocks = gram_tile(place, [own, across, *other], cols[1], depth)
    last = blocks[0]
    for d in (4, 3, 5, 2, 6, 1, 7):
        last = last + shifted(blocks[d], "z", d).astype(jnp.float32)
    return jnp.concatenate([total, last], axis=1)


def solution(mesh):
    fine = Mesh(mesh.devices.reshape(2, 4, 8, 2, 2), CELLS + TRACERS)
    placed = (
        P(TRACERS, CELLS, None),
        P(CELLS, None),
        P(CELLS, None),
        P(CELLS, None),
        P(CELLS, None),
        P(CELLS),
    )
    return jax.shard_map(
        on_device, mesh=fine, in_specs=placed, out_specs=P(CELLS, TRACERS), check_vma=False
    )
```

profile of v0, /device:TPU:4, one launch (start us, length us, event | category | flops | bytes accessed | tf_op | source)
XLA Modules:
  0.0 143.7 jit_solution(16877749494910562179)
XLA Ops:
  0.0 2.5 %edges.1 = (bf16[2320,128]{1,0:T(8,128)(2,1)S(1)}, bf16[2320,128]{1,0:T(8,128)(2,1)S(1)}, bf16[784,128]{1,0:T(8,128)(2,1)}, bf16[784,128]{1,0:T(8,128)(2,1)}) custom-call(f32[4096,128]{1,0:T(8,128)} %bitcast.47, f32[4,128]{1,0:T(4,128)} %wind_x_ref.5, f32[4,128]{1,0:T(4,128)} %wind_y_ref.5), custom_call_target="tpu_custom_call" | custom-call | tf_op jit(solution)/shard_map/edges/pallas_call | solution.py:77
  2.5 2.0 %collective-permute-start.2 = (bf16[2320,128]{1,0:T(8,128)(2,1)S(1)}, bf16[2320,128]{1,0:T(8,128)(2,1)S(1)}, u32[]{:S(2)}, u32[]{:S(2)}) collective-permute-start(bf16[2320,128]{1,0:T(8,128)(2,1)S(1)} %get-tuple-element.23), channel_id=1, source_target_pairs={{0,4},{4,8},{8,12},{12,16},{16,20},{20,24},{24,28},{28,32},{32,36}... | collective-permute-start | bytes 1781768 | tf_op jit(solution)/shard_map/ppermute | solution.py:23
  4.5 7.1 %collective-permute-start.3 = (bf16[2320,128]{1,0:T(8,128)(2,1)S(1)}, bf16[2320,128]{1,0:T(8,128)(2,1)S(1)}, u32[]{:S(2)}, u32[]{:S(2)}) collective-permute-start(bf16[2320,128]{1,0:T(8,128)(2,1)S(1)} %get-tuple-element.24), channel_id=1, source_target_pairs={{0,252},{4,0},{8,4},{12,8},{16,12},{20,16},{24,20},{28,24},{32,28}... | collective-permute-start | bytes 1781768 | tf_op jit(solution)/shard_map/ppermute | solution.py:23
  11.6 0.2 convert_reduce_fusion.2
  11.8 0.1 convert_reduce_fusion.1
  11.9 0.1 fusion.8
  12.1 0.1 iota_compare_fusion
  12.2 1.1 fusion
  13.3 6.9 %all-to-all-start = ((bf16[64,8,256]{2,1,0:T(8,128)(2,1)}), bf16[64,8,256]{2,1,0:T(8,128)(2,1)S(1)}, u32[]{:S(2)}, u32[]{:S(2)}) async-start(bf16[64,8,256]{2,1,0:T(8,128)(2,1)} %fusion), calls=%async_computation | async-start | bytes 524288 | tf_op jit(solution)/shard_map/all_to_all | solution.py:27
  20.2 1.6 %collective-permute-start = (bf16[784,128]{1,0:T(8,128)(2,1)}, bf16[784,128]{1,0:T(8,128)(2,1)S(1)}, u32[]{:S(2)}, u32[]{:S(2)}) collective-permute-start(bf16[784,128]{1,0:T(8,128)(2,1)} %get-tuple-element.21), channel_id=1, source_target_pairs={{0,4},{4,8},{8,12},{12,16},{16,20},{20,24},{24,28},{28,32},{32,36}... | collective-permute-start | bytes 602120 | tf_op jit(solution)/shard_map/ppermute | solution.py:23
  21.9 4.7 %collective-permute-start.1 = (bf16[784,128]{1,0:T(8,128)(2,1)}, bf16[784,128]{1,0:T(8,128)(2,1)S(1)}, u32[]{:S(2)}, u32[]{:S(2)}) collective-permute-start(bf16[784,128]{1,0:T(8,128)(2,1)} %get-tuple-element.22), channel_id=1, source_target_pairs={{0,252},{4,0},{8,4},{12,8},{16,12},{20,16},{24,20},{28,24},{32,28}... | collective-permute-start | bytes 602120 | tf_op jit(solution)/shard_map/ppermute | solution.py:23
  26.5 0.1 stack.71.place_ref
  26.7 2.3 %collective-permute-done.3.b0.b1.b2.b_winds = bf16[2320,128]{1,0:T(8,128)(2,1)S(1)} collective-permute-done((bf16[2320,128]{1,0:T(8,128)(2,1)S(1)}, bf16[2320,128]{1,0:T(8,128)(2,1)S(1)}, u32[]{:S(2)}, u32[]{:S(2)}) %collective-permute-start.3) | collective-permute-done | bytes 593952 | tf_op jit(solution)/shard_map/ppermute | solution.py:23
  28.9 5.0 %transport.2.refs_0_ = bf16[1024,512]{1,0:T(8,128)(2,1)S(1)} custom-call(f32[4096,128]{1,0:T(8,128)} %bitcast.48, bf16[2320,128]{1,0:T(8,128)(2,1)S(1)} %collective-permute-done.2.a0.a1.a2.a_winds, bf16[2320,128]{1,0:T(8,128)(2,1)S(1)} %collective-permute-done.2.a0.a1.a2.a_winds, bf16[2320,128]{1,0:T(8,128)(2,1)S(1)} %collective-permute-done.2.a0.a1.a2.a_winds, ...), custom_call_target="tpu_custom_call" | custom-call | tf_op jit(solution)/shard_map/transport/pallas_call | solution.py:161
  34.0 1.7 %collective-permute-done.a0.a1.a2.a_winds = bf16[784,128]{1,0:T(8,128)(2,1)S(1)} collective-permute-done((bf16[784,128]{1,0:T(8,128)(2,1)}, bf16[784,128]{1,0:T(8,128)(2,1)S(1)}, u32[]{:S(2)}, u32[]{:S(2)}) %collective-permute-start) | collective-permute-done | bytes 200736 | tf_op jit(solution)/shard_map/ppermute | solution.py:23
  35.6 2.2 %transport.3.low_ref.high_ref = bf16[1024,512]{1,0:T(8,128)(2,1)S(1)} custom-call(f32[4096,128]{1,0:T(8,128)} %bitcast.49, bf16[784,128]{1,0:T(8,128)(2,1)S(1)} %collective-permute-done.a0.a1.a2.a_winds, bf16[784,128]{1,0:T(8,128)(2,1)S(1)} %collective-permute-done.a0.a1.a2.a_winds, ...), custom_call_target="tpu_custom_call", output_to_operand_aliasing={{}: (11, {})} | custom-call | tf_op jit(solution)/shard_map/transport/pallas_call | solution.py:161
  37.9 1.1 jacobian.1
  39.0 25.2 %all_to_all.15 = bf16[64,8,512]{2,1,0:T(8,128)(2,1)S(1)} all-to-all(bf16[64,8,512]{2,1,0:T(8,128)(2,1)S(1)} %bitcast.45), channel_id=1, replica_groups=mesh['xl'=2,'y'=4,'z'=8,'xh'=2,'core'=2] {'xl','y','z'}, dimensions={0} | all-to-all | bytes 1048576 | tf_op jit(solution)/shard_map/all_to_all | solution.py:27
  64.3 0.3 fusion.3
  64.5 0.3 broadcast_select_fusion
  64.8 2.9 %collective-permute-start.4 = (bf16[128,512]{1,0:T(8,128)(2,1)S(1)}, bf16[128,512]{1,0:T(8,128)(2,1)S(1)}, u32[]{:S(2)}, u32[]{:S(2)}) collective-permute-start(bf16[128,512]{1,0:T(8,128)(2,1)S(1)} %get-tuple-element.38), channel_id=1, source_target_pairs={{0,0},{1,64},{2,128},{3,192},{32,32},{33,96},{34,160},{35,224},{64... | collective-permute-start | bytes 393224 | tf_op jit(solution)/shard_map/ppermute | solution.py:333
  67.7 1.2 collective-permute-start.5
  68.9 0.1 multiply_convert_fusion.1
  69.0 3.6 %collective-permute-done.4 = bf16[128,512]{1,0:T(8,128)(2,1)S(1)} collective-permute-done((bf16[128,512]{1,0:T(8,128)(2,1)S(1)}, bf16[128,512]{1,0:T(8,128)(2,1)S(1)}, u32[]{:S(2)}, u32[]{:S(2)}) %collective-permute-start.4) | collective-permute-done | bytes 131104 | tf_op jit(solution)/shard_map/ppermute | solution.py:333
  72.7 2.4 %collective-permute-done.5 = bf16[128,512]{1,0:T(8,128)(2,1)S(1)} collective-permute-done((bf16[128,512]{1,0:T(8,128)(2,1)S(1)}, bf16[128,512]{1,0:T(8,128)(2,1)S(1)}, u32[]{:S(2)}, u32[]{:S(2)}) %collective-permute-start.5) | collective-permute-done | bytes 131104 | tf_op jit(solution)/shard_map/ppermute | solution.py:334
  75.1 0.1 collective-permute-start.6
  75.2 3.9 %collective-permute-start.9 = (bf16[128,640]{1,0:T(8,128)(2,1)S(1)}, bf16[128,640]{1,0:T(8,128)(2,1)S(1)}, u32[]{:S(2)}, u32[]{:S(2)}) collective-permute-start(bf16[128,640]{1,0:T(8,128)(2,1)S(1)} %pad_maximum_fusion.1.refs_4_), channel_id=1, source_target_pairs={{0,128},{128,0},{1,129},{129,1},{2,130},{130,2},{3,131},{131,3},{4... | collective-permute-start | bytes 491528 | tf_op jit(solution)/shard_map/ppermute | solution.py:23
  79.1 0.6 collective-permute-start.10
  79.7 1.7 %collective-permute-start.11 = (bf16[128,640]{1,0:T(8,128)(2,1)S(1)}, bf16[128,640]{1,0:T(8,128)(2,1)S(1)}, u32[]{:S(2)}, u32[]{:S(2)}) collective-permute-start(bf16[128,640]{1,0:T(8,128)(2,1)S(1)} %pad_maximum_fusion.1.refs_4_), channel_id=1, source_target_pairs={{0,64},{32,96},{64,0},{96,32},{1,65},{33,97},{65,1},{97,33},{2,66}... | collective-permute-start | bytes 491528 | tf_op jit(solution)/shard_map/ppermute | solution.py:23
  81.4 2.3 %collective-permute-start.12 = (bf16[128,640]{1,0:T(8,128)(2,1)S(1)}, bf16[128,640]{1,0:T(8,128)(2,1)S(1)}, u32[]{:S(2)}, u32[]{:S(2)}) collective-permute-start(bf16[128,640]{1,0:T(8,128)(2,1)S(1)} %pad_maximum_fusion.1.refs_4_), channel_id=1, source_target_pairs={{0,96},{32,0},{64,32},{96,64},{1,97},{33,1},{65,33},{97,65},{2,98}... | collective-permute-start | bytes 491528 | tf_op jit(solution)/shard_map/ppermute | solution.py:23
  83.7 4.5 %collective-permute-done.9.refs_5_ = bf16[128,640]{1,0:T(8,128)(2,1)S(1)} collective-permute-done((bf16[128,640]{1,0:T(8,128)(2,1)S(1)}, bf16[128,640]{1,0:T(8,128)(2,1)S(1)}, u32[]{:S(2)}, u32[]{:S(2)}) %collective-permute-start.9) | collective-permute-done | bytes 163872 | tf_op jit(solution)/shard_map/ppermute | solution.py:23
  88.2 1.6 %collective-permute-start.7 = (bf16[256,512]{1,0:T(8,128)(2,1)S(1)}, bf16[256,512]{1,0:T(8,128)(2,1)S(1)}, u32[]{:S(2)}, u32[]{:S(2)}) collective-permute-start(bf16[256,512]{1,0:T(8,128)(2,1)S(1)} %constant_dynamic-update-slice_fusion.refs_0_), channel_id=1, source_target_pairs={{0,1},{1,0},{2,3},{3,2},{4,5},{5,4},{6,7},{7,6},{8,9},{9,8},{10,11... | collective-permute-start | bytes 786440 | tf_op jit(solution)/shard_map/ppermute | solution.py:23
  89.8 0.2 collective-permute-done.10.refs_6_
  90.0 0.4 collective-permute-start.13
  90.4 0.7 collective-permute-start.14
  91.1 0.1 collective-permute-done.12.refs_8_
  91.2 3.3 %collective-permute-start.15 = (bf16[128,640]{1,0:T(8,128)(2,1)S(1)}, bf16[128,640]{1,0:T(8,128)(2,1)S(1)}, u32[]{:S(2)}, u32[]{:S(2)}) collective-permute-start(bf16[128,640]{1,0:T(8,128)(2,1)S(1)} %collective-permute-done.9.refs_5_), channel_id=1, source_target_pairs={{0,96},{32,0},{64,32},{96,64},{1,97},{33,1},{65,33},{97,65},{2,98}... | collective-permute-start | bytes 491528 | tf_op jit(solution)/shard_map/ppermute | solution.py:23
  94.4 7.1 %collective-permute-done.13.refs_9_ = bf16[128,640]{1,0:T(8,128)(2,1)S(1)} collective-permute-done((bf16[128,640]{1,0:T(8,128)(2,1)S(1)}, bf16[128,640]{1,0:T(8,128)(2,1)S(1)}, u32[]{:S(2)}, u32[]{:S(2)}) %collective-permute-start.13) | collective-permute-done | bytes 163872 | tf_op jit(solution)/shard_map/ppermute | solution.py:23
  101.5 0.6 collective-permute-done.15.refs_11_
  102.2 2.8 %gram.2 = bf16[512,640]{1,0:T(8,128)(2,1)} custom-call(s32[17]{0:T(128)S(1)} %stack.71.place_ref, bf16[256,512]{1,0:T(8,128)(2,1)S(1)} %constant_dynamic-update-slice_fusion.refs_0_, bf16[256,512]{1,0:T(8,128)(2,1)S(1)} %collective-permute-done.6.refs_1_, bf16[256,512]{1,0:T(8,128)(2,1)S(1)} %collective-permute-done.7.refs_2_, ...), custom_call_target="tpu_custom_call" | custom-call | tf_op jit(solution)/shard_map/gram/pallas_call | solution.py:253
  105.0 3.5 %all-to-all-start.2 = ((bf16[8,64,640]{2,1,0:T(8,128)(2,1)}), bf16[8,64,640]{2,1,0:T(8,128)(2,1)S(1)}, u32[]{:S(2)}, u32[]{:S(2)}) async-start(bf16[8,64,640]{2,1,0:T(8,128)(2,1)} %bitcast.28), calls=%async_computation.2 | async-start | bytes 1310720 | tf_op jit(solution)/shard_map/all_to_all | solution.py:27
  108.5 0.2 collective-permute-start.16
  108.7 0.2 collective-permute-start.17
  108.9 3.9 %collective-permute-start.18 = (bf16[128,384]{1,0:T(8,128)(2,1)S(1)}, bf16[128,384]{1,0:T(8,128)(2,1)S(1)}, u32[]{:S(2)}, u32[]{:S(2)}) collective-permute-start(bf16[128,384]{1,0:T(8,128)(2,1)S(1)} %slice.18.refs_4_), channel_id=1, source_target_pairs={{0,64},{32,96},{64,0},{96,32},{1,65},{33,97},{65,1},{97,33},{2,66}... | collective-permute-start | bytes 294920 | tf_op jit(solution)/shard_map/ppermute | solution.py:23
  112.8 0.4 collective-permute-done.16.refs_5_
  113.2 1.6 %collective-permute-start.20 = (bf16[128,384]{1,0:T(8,128)(2,1)S(1)}, bf16[128,384]{1,0:T(8,128)(2,1)S(1)}, u32[]{:S(2)}, u32[]{:S(2)}) collective-permute-start(bf16[128,384]{1,0:T(8,128)(2,1)S(1)} %collective-permute-done.16.refs_5_), channel_id=1, source_target_pairs={{0,32},{32,64},{64,96},{96,0},{1,33},{33,65},{65,97},{97,1},{2,34}... | collective-permute-start | bytes 294920 | tf_op jit(solution)/shard_map/ppermute | solution.py:23
  114.8 2.6 %collective-permute-start.21 = (bf16[128,384]{1,0:T(8,128)(2,1)S(1)}, bf16[128,384]{1,0:T(8,128)(2,1)S(1)}, u32[]{:S(2)}, u32[]{:S(2)}) collective-permute-start(bf16[128,384]{1,0:T(8,128)(2,1)S(1)} %collective-permute-done.16.refs_5_), channel_id=1, source_target_pairs={{0,64},{32,96},{64,0},{96,32},{1,65},{33,97},{65,1},{97,33},{2,66}... | collective-permute-start | bytes 294920 | tf_op jit(solution)/shard_map/ppermute | solution.py:23
  117.4 0.1 collective-permute-start.22
  117.5 0.5 collective-permute-done.18.refs_7_
  118.0 0.3 collective-permute-done.19.refs_8_
  118.3 2.2 %collective-permute-done.20.refs_9_ = bf16[128,384]{1,0:T(8,128)(2,1)S(1)} collective-permute-done((bf16[128,384]{1,0:T(8,128)(2,1)S(1)}, bf16[128,384]{1,0:T(8,128)(2,1)S(1)}, u32[]{:S(2)}, u32[]{:S(2)}) %collective-permute-start.20) | collective-permute-done | bytes 98336 | tf_op jit(solution)/shard_map/ppermute | solution.py:23
  120.6 1.2 collective-permute-done.21.refs_10_
  121.8 0.2 collective-permute-done.22.refs_11_
  122.1 1.7 %gram.3 = (f32[64,384]{1,0:T(8,128)S(1)}, bf16[64,384]{1,0:T(8,128)(2,1)S(1)}, bf16[64,384]{1,0:T(8,128)(2,1)S(1)}, bf16[64,384]{1,0:T(8,128)(2,1)S(1)}, bf16[64...) custom-call(s32[17]{0:T(128)S(1)} %stack.71.place_ref, ...), custom_call_target="tpu_custom_call" | custom-call | tf_op jit(solution)/shard_map/gram/pallas_call | solution.py:253
  123.7 3.1 %collective-permute-start.29 = (bf16[64,384]{1,0:T(8,128)(2,1)S(1)}, bf16[64,384]{1,0:T(8,128)(2,1)S(1)}, u32[]{:S(2)}, u32[]{:S(2)}) collective-permute-start(bf16[64,384]{1,0:T(8,128)(2,1)S(1)} %get-tuple-element.36), channel_id=1, source_target_pairs={{0,28},{4,0},{8,4},{12,8},{16,12},{20,16},{24,20},{28,24},{1,29},{... | collective-permute-start | bytes 147464 | tf_op jit(solution)/shard_map/ppermute | solution.py:23
  126.9 2.9 %collective-permute-start.27 = (bf16[64,384]{1,0:T(8,128)(2,1)S(1)}, bf16[64,384]{1,0:T(8,128)(2,1)S(1)}, u32[]{:S(2)}, u32[]{:S(2)}) collective-permute-start(bf16[64,384]{1,0:T(8,128)(2,1)S(1)} %get-tuple-element.34), channel_id=1, source_target_pairs={{0,24},{4,28},{8,0},{12,4},{16,8},{20,12},{24,16},{28,20},{1,25},{... | collective-permute-start | bytes 147464 | tf_op jit(solution)/shard_map/ppermute | solution.py:23
  129.8 3.8 %collective-permute-start.25 = (bf16[64,384]{1,0:T(8,128)(2,1)S(1)}, bf16[64,384]{1,0:T(8,128)(2,1)S(1)}, u32[]{:S(2)}, u32[]{:S(2)}) collective-permute-start(bf16[64,384]{1,0:T(8,128)(2,1)S(1)} %get-tuple-element.32), channel_id=1, source_target_pairs={{0,20},{4,24},{8,28},{12,0},{16,4},{20,8},{24,12},{28,16},{1,21},{... | collective-permute-start | bytes 147464 | tf_op jit(solution)/shard_map/ppermute | solution.py:23
  133.6 1.2 collective-permute-start.24
  134.8 3.5 %collective-permute-start.23 = (bf16[64,384]{1,0:T(8,128)(2,1)S(1)}, bf16[64,384]{1,0:T(8,128)(2,1)S(1)}, u32[]{:S(2)}, u32[]{:S(2)}) collective-permute-start(bf16[64,384]{1,0:T(8,128)(2,1)S(1)} %get-tuple-element.30), channel_id=1, source_target_pairs={{0,16},{4,20},{8,24},{12,28},{16,0},{20,4},{24,8},{28,12},{1,17},{... | collective-permute-start | bytes 147464 | tf_op jit(solution)/shard_map/ppermute | solution.py:23
  138.3 3.4 %collective-permute-done.24 = bf16[64,384]{1,0:T(8,128)(2,1)S(1)} collective-permute-done((bf16[64,384]{1,0:T(8,128)(2,1)S(1)}, bf16[64,384]{1,0:T(8,128)(2,1)S(1)}, u32[]{:S(2)}, u32[]{:S(2)}) %collective-permute-start.24) | collective-permute-done | bytes 49184 | tf_op jit(solution)/shard_map/ppermute | solution.py:23
  141.7 1.1 collective-permute-done.23
  142.8 0.1 convert_add_fusion
  142.9 0.1 convert_reduce_fusion
  143.0 0.7 pad_maximum_fusion
  (36 shorter events, 0.1 us)
Async XLA Ops:
  0.0 11.6 %copy-start.3 = (s32[128,1]{0,1:T(1,128)S(1)}, s32[128,1]{0,1:T(1,128)}, u32[]{:S(2)}) copy-start(s32[128,1]{0,1:T(1,128)} %param.9) | copy-start | bytes 1540
  0.0 11.8 %copy-start.2 = (bf16[128,512]{1,0:T(8,128)(2,1)S(1)}, bf16[128,512]{1,0:T(8,128)(2,1)}, u32[]{:S(2)}) copy-start(bf16[128,512]{1,0:T(8,128)(2,1)} %param.10) | copy-start | bytes 393220
  0.0 26.6 %copy-start.4 = (bf16[128]{0:T(256)(128)(2,1)S(1)}, bf16[128]{0:T(256)(128)(2,1)}, u32[]{:S(2)}) copy-start(bf16[128]{0:T(256)(128)(2,1)} %param.11) | copy-start | bytes 772
  0.0 28.9 %copy-start = (f32[4,128]{1,0:T(4,128)S(1)}, f32[4,128]{1,0:T(4,128)}, u32[]{:S(2)}) copy-start(f32[4,128]{1,0:T(4,128)} %wind_x_ref.5) | copy-start | bytes 6148
  0.0 28.9 %copy-start.1 = (f32[4,128]{1,0:T(4,128)S(1)}, f32[4,128]{1,0:T(4,128)}, u32[]{:S(2)}) copy-start(f32[4,128]{1,0:T(4,128)} %wind_y_ref.5) | copy-start | bytes 6148
  2.5 24.1 %collective-permute-start.2 = (bf16[2320,128]{1,0:T(8,128)(2,1)S(1)}, bf16[2320,128]{1,0:T(8,128)(2,1)S(1)}, u32[]{:S(2)}, u32[]{:S(2)}) collective-permute-start(bf16[2320,128]{1,0:T(8,128)(2,1)S(1)} %get-tuple-element.23), channel_id=1, source_target_pairs={{0,4},{4,8},{8,12},{12,16},{16,20},{20,24},{24,28},{28,32},{32,36}... | collective-permute-start | bytes 1781768 | tf_op jit(solution)/shard_map/ppermute | solution.py:23
  4.5 24.4 %collective-permute-start.3 = (bf16[2320,128]{1,0:T(8,128)(2,1)S(1)}, bf16[2320,128]{1,0:T(8,128)(2,1)S(1)}, u32[]{:S(2)}, u32[]{:S(2)}) collective-permute-start(bf16[2320,128]{1,0:T(8,128)(2,1)S(1)} %get-tuple-element.24), channel_id=1, source_target_pairs={{0,252},{4,0},{8,4},{12,8},{16,12},{20,16},{24,20},{28,24},{32,28}... | collective-permute-start | bytes 1781768 | tf_op jit(solution)/shard_map/ppermute | solution.py:23
  13.3 24.6 %all-to-all-start = ((bf16[64,8,256]{2,1,0:T(8,128)(2,1)}), bf16[64,8,256]{2,1,0:T(8,128)(2,1)S(1)}, u32[]{:S(2)}, u32[]{:S(2)}) async-start(bf16[64,8,256]{2,1,0:T(8,128)(2,1)} %fusion), calls=%async_computation | async-start | bytes 524288 | tf_op jit(solution)/shard_map/all_to_all | solution.py:27
  20.2 15.4 %collective-permute-start = (bf16[784,128]{1,0:T(8,128)(2,1)}, bf16[784,128]{1,0:T(8,128)(2,1)S(1)}, u32[]{:S(2)}, u32[]{:S(2)}) collective-permute-start(bf16[784,128]{1,0:T(8,128)(2,1)} %get-tuple-element.21), channel_id=1, source_target_pairs={{0,4},{4,8},{8,12},{12,16},{16,20},{20,24},{24,28},{28,32},{32,36}... | collective-permute-start | bytes 602120 | tf_op jit(solution)/shard_map/ppermute | solution.py:23
  21.9 13.8 %collective-permute-start.1 = (bf16[784,128]{1,0:T(8,128)(2,1)}, bf16[784,128]{1,0:T(8,128)(2,1)S(1)}, u32[]{:S(2)}, u32[]{:S(2)}) collective-permute-start(bf16[784,128]{1,0:T(8,128)(2,1)} %get-tuple-element.22), channel_id=1, source_target_pairs={{0,252},{4,0},{8,4},{12,8},{16,12},{20,16},{24,20},{28,24},{32,28}... | collective-permute-start | bytes 602120 | tf_op jit(solution)/shard_map/ppermute | solution.py:23
  64.8 7.8 %collective-permute-start.4 = (bf16[128,512]{1,0:T(8,128)(2,1)S(1)}, bf16[128,512]{1,0:T(8,128)(2,1)S(1)}, u32[]{:S(2)}, u32[]{:S(2)}) collective-permute-start(bf16[128,512]{1,0:T(8,128)(2,1)S(1)} %get-tuple-element.38), channel_id=1, source_target_pairs={{0,0},{1,64},{2,128},{3,192},{32,32},{33,96},{34,160},{35,224},{64... | collective-permute-start | bytes 393224 | tf_op jit(solution)/shard_map/ppermute | solution.py:333
  67.7 7.4 %collective-permute-start.5 = (bf16[128,512]{1,0:T(8,128)(2,1)S(1)}, bf16[128,512]{1,0:T(8,128)(2,1)S(1)}, u32[]{:S(2)}, u32[]{:S(2)}) collective-permute-start(bf16[128,512]{1,0:T(8,128)(2,1)S(1)} %get-tuple-element.37), channel_id=1, source_target_pairs={{0,32},{1,96},{2,160},{3,224},{32,0},{33,64},{34,128},{35,192},{64... | collective-permute-start | bytes 393224 | tf_op jit(solution)/shard_map/ppermute | solution.py:334
  75.1 14.7 %collective-permute-start.6 = (bf16[256,512]{1,0:T(8,128)(2,1)S(1)}, bf16[256,512]{1,0:T(8,128)(2,1)S(1)}, u32[]{:S(2)}, u32[]{:S(2)}) collective-permute-start(bf16[256,512]{1,0:T(8,128)(2,1)S(1)} %constant_dynamic-update-slice_fusion.refs_0_), channel_id=1, source_target_pairs={{0,2},{2,0},{1,3},{3,1},{4,6},{6,4},{5,7},{7,5},{8,10},{10,8},{9,1... | collective-permute-start | bytes 786440 | tf_op jit(solution)/shard_map/ppermute | solution.py:23
  75.2 12.9 %collective-permute-start.9 = (bf16[128,640]{1,0:T(8,128)(2,1)S(1)}, bf16[128,640]{1,0:T(8,128)(2,1)S(1)}, u32[]{:S(2)}, u32[]{:S(2)}) collective-permute-start(bf16[128,640]{1,0:T(8,128)(2,1)S(1)} %pad_maximum_fusion.1.refs_4_), channel_id=1, source_target_pairs={{0,128},{128,0},{1,129},{129,1},{2,130},{130,2},{3,131},{131,3},{4... | collective-permute-start | bytes 491528 | tf_op jit(solution)/shard_map/ppermute | solution.py:23
  79.1 10.9 %collective-permute-start.10 = (bf16[128,640]{1,0:T(8,128)(2,1)S(1)}, bf16[128,640]{1,0:T(8,128)(2,1)S(1)}, u32[]{:S(2)}, u32[]{:S(2)}) collective-permute-start(bf16[128,640]{1,0:T(8,128)(2,1)S(1)} %pad_maximum_fusion.1.refs_4_), channel_id=1, source_target_pairs={{0,32},{32,64},{64,96},{96,0},{1,33},{33,65},{65,97},{97,1},{2,34}... | collective-permute-start | bytes 491528 | tf_op jit(solution)/shard_map/ppermute | solution.py:23
  79.7 10.8 %collective-permute-start.11 = (bf16[128,640]{1,0:T(8,128)(2,1)S(1)}, bf16[128,640]{1,0:T(8,128)(2,1)S(1)}, u32[]{:S(2)}, u32[]{:S(2)}) collective-permute-start(bf16[128,640]{1,0:T(8,128)(2,1)S(1)} %pad_maximum_fusion.1.refs_4_), channel_id=1, source_target_pairs={{0,64},{32,96},{64,0},{96,32},{1,65},{33,97},{65,1},{97,33},{2,66}... | collective-permute-start | bytes 491528 | tf_op jit(solution)/shard_map/ppermute | solution.py:23
  81.4 9.8 %collective-permute-start.12 = (bf16[128,640]{1,0:T(8,128)(2,1)S(1)}, bf16[128,640]{1,0:T(8,128)(2,1)S(1)}, u32[]{:S(2)}, u32[]{:S(2)}) collective-permute-start(bf16[128,640]{1,0:T(8,128)(2,1)S(1)} %pad_maximum_fusion.1.refs_4_), channel_id=1, source_target_pairs={{0,96},{32,0},{64,32},{96,64},{1,97},{33,1},{65,33},{97,65},{2,98}... | collective-permute-start | bytes 491528 | tf_op jit(solution)/shard_map/ppermute | solution.py:23
  88.2 14.0 %collective-permute-start.7 = (bf16[256,512]{1,0:T(8,128)(2,1)S(1)}, bf16[256,512]{1,0:T(8,128)(2,1)S(1)}, u32[]{:S(2)}, u32[]{:S(2)}) collective-permute-start(bf16[256,512]{1,0:T(8,128)(2,1)S(1)} %constant_dynamic-update-slice_fusion.refs_0_), channel_id=1, source_target_pairs={{0,1},{1,0},{2,3},{3,2},{4,5},{5,4},{6,7},{7,6},{8,9},{9,8},{10,11... | collective-permute-start | bytes 786440 | tf_op jit(solution)/shard_map/ppermute | solution.py:23
  89.8 12.4 %collective-permute-start.8 = (bf16[256,512]{1,0:T(8,128)(2,1)S(1)}, bf16[256,512]{1,0:T(8,128)(2,1)S(1)}, u32[]{:S(2)}, u32[]{:S(2)}) collective-permute-start(bf16[256,512]{1,0:T(8,128)(2,1)S(1)} %collective-permute-done.6.refs_1_), channel_id=1, source_target_pairs={{0,1},{1,0},{2,3},{3,2},{4,5},{5,4},{6,7},{7,6},{8,9},{9,8},{10,11... | collective-permute-start | bytes 786440 | tf_op jit(solution)/shard_map/ppermute | solution.py:23
  90.0 11.6 %collective-permute-start.13 = (bf16[128,640]{1,0:T(8,128)(2,1)S(1)}, bf16[128,640]{1,0:T(8,128)(2,1)S(1)}, u32[]{:S(2)}, u32[]{:S(2)}) collective-permute-start(bf16[128,640]{1,0:T(8,128)(2,1)S(1)} %collective-permute-done.9.refs_5_), channel_id=1, source_target_pairs={{0,32},{32,64},{64,96},{96,0},{1,33},{33,65},{65,97},{97,1},{2,34}... | collective-permute-start | bytes 491528 | tf_op jit(solution)/shard_map/ppermute | solution.py:23
  90.4 11.1 %collective-permute-start.14 = (bf16[128,640]{1,0:T(8,128)(2,1)S(1)}, bf16[128,640]{1,0:T(8,128)(2,1)S(1)}, u32[]{:S(2)}, u32[]{:S(2)}) collective-permute-start(bf16[128,640]{1,0:T(8,128)(2,1)S(1)} %collective-permute-done.9.refs_5_), channel_id=1, source_target_pairs={{0,64},{32,96},{64,0},{96,32},{1,65},{33,97},{65,1},{97,33},{2,66}... | collective-permute-start | bytes 491528 | tf_op jit(solution)/shard_map/ppermute | solution.py:23
  91.2 11.0 %collective-permute-start.15 = (bf16[128,640]{1,0:T(8,128)(2,1)S(1)}, bf16[128,640]{1,0:T(8,128)(2,1)S(1)}, u32[]{:S(2)}, u32[]{:S(2)}) collective-permute-start(bf16[128,640]{1,0:T(8,128)(2,1)S(1)} %collective-permute-done.9.refs_5_), channel_id=1, source_target_pairs={{0,96},{32,0},{64,32},{96,64},{1,97},{33,1},{65,33},{97,65},{2,98}... | collective-permute-start | bytes 491528 | tf_op jit(solution)/shard_map/ppermute | solution.py:23
  105.0 37.9 %all-to-all-start.2 = ((bf16[8,64,640]{2,1,0:T(8,128)(2,1)}), bf16[8,64,640]{2,1,0:T(8,128)(2,1)S(1)}, u32[]{:S(2)}, u32[]{:S(2)}) async-start(bf16[8,64,640]{2,1,0:T(8,128)(2,1)} %bitcast.28), calls=%async_computation.2 | async-start | bytes 1310720 | tf_op jit(solution)/shard_map/all_to_all | solution.py:27
  108.5 4.7 %collective-permute-start.16 = (bf16[128,384]{1,0:T(8,128)(2,1)S(1)}, bf16[128,384]{1,0:T(8,128)(2,1)S(1)}, u32[]{:S(2)}, u32[]{:S(2)}) collective-permute-start(bf16[128,384]{1,0:T(8,128)(2,1)S(1)} %slice.18.refs_4_), channel_id=1, source_target_pairs={{0,128},{128,0},{1,129},{129,1},{2,130},{130,2},{3,131},{131,3},{4... | collective-permute-start | bytes 294920 | tf_op jit(solution)/shard_map/ppermute | solution.py:23
  108.7 8.7 %collective-permute-start.17 = (bf16[128,384]{1,0:T(8,128)(2,1)S(1)}, bf16[128,384]{1,0:T(8,128)(2,1)S(1)}, u32[]{:S(2)}, u32[]{:S(2)}) collective-permute-start(bf16[128,384]{1,0:T(8,128)(2,1)S(1)} %slice.18.refs_4_), channel_id=1, source_target_pairs={{0,32},{32,64},{64,96},{96,0},{1,33},{33,65},{65,97},{97,1},{2,34}... | collective-permute-start | bytes 294920 | tf_op jit(solution)/shard_map/ppermute | solution.py:23
  108.9 9.1 %collective-permute-start.18 = (bf16[128,384]{1,0:T(8,128)(2,1)S(1)}, bf16[128,384]{1,0:T(8,128)(2,1)S(1)}, u32[]{:S(2)}, u32[]{:S(2)}) collective-permute-start(bf16[128,384]{1,0:T(8,128)(2,1)S(1)} %slice.18.refs_4_), channel_id=1, source_target_pairs={{0,64},{32,96},{64,0},{96,32},{1,65},{33,97},{65,1},{97,33},{2,66}... | collective-permute-start | bytes 294920 | tf_op jit(solution)/shard_map/ppermute | solution.py:23
  112.8 5.5 %collective-permute-start.19 = (bf16[128,384]{1,0:T(8,128)(2,1)S(1)}, bf16[128,384]{1,0:T(8,128)(2,1)S(1)}, u32[]{:S(2)}, u32[]{:S(2)}) collective-permute-start(bf16[128,384]{1,0:T(8,128)(2,1)S(1)} %slice.18.refs_4_), channel_id=1, source_target_pairs={{0,96},{32,0},{64,32},{96,64},{1,97},{33,1},{65,33},{97,65},{2,98}... | collective-permute-start | bytes 294920 | tf_op jit(solution)/shard_map/ppermute | solution.py:23
  113.2 7.3 %collective-permute-start.20 = (bf16[128,384]{1,0:T(8,128)(2,1)S(1)}, bf16[128,384]{1,0:T(8,128)(2,1)S(1)}, u32[]{:S(2)}, u32[]{:S(2)}) collective-permute-start(bf16[128,384]{1,0:T(8,128)(2,1)S(1)} %collective-permute-done.16.refs_5_), channel_id=1, source_target_pairs={{0,32},{32,64},{64,96},{96,0},{1,33},{33,65},{65,97},{97,1},{2,34}... | collective-permute-start | bytes 294920 | tf_op jit(solution)/shard_map/ppermute | solution.py:23
  114.8 7.0 %collective-permute-start.21 = (bf16[128,384]{1,0:T(8,128)(2,1)S(1)}, bf16[128,384]{1,0:T(8,128)(2,1)S(1)}, u32[]{:S(2)}, u32[]{:S(2)}) collective-permute-start(bf16[128,384]{1,0:T(8,128)(2,1)S(1)} %collective-permute-done.16.refs_5_), channel_id=1, source_target_pairs={{0,64},{32,96},{64,0},{96,32},{1,65},{33,97},{65,1},{97,33},{2,66}... | collective-permute-start | bytes 294920 | tf_op jit(solution)/shard_map/ppermute | solution.py:23
  117.4 4.6 %collective-permute-start.22 = (bf16[128,384]{1,0:T(8,128)(2,1)S(1)}, bf16[128,384]{1,0:T(8,128)(2,1)S(1)}, u32[]{:S(2)}, u32[]{:S(2)}) collective-permute-start(bf16[128,384]{1,0:T(8,128)(2,1)S(1)} %collective-permute-done.16.refs_5_), channel_id=1, source_target_pairs={{0,96},{32,0},{64,32},{96,64},{1,97},{33,1},{65,33},{97,65},{2,98}... | collective-permute-start | bytes 294920 | tf_op jit(solution)/shard_map/ppermute | solution.py:23
  123.7 9.9 %collective-permute-start.29 = (bf16[64,384]{1,0:T(8,128)(2,1)S(1)}, bf16[64,384]{1,0:T(8,128)(2,1)S(1)}, u32[]{:S(2)}, u32[]{:S(2)}) collective-permute-start(bf16[64,384]{1,0:T(8,128)(2,1)S(1)} %get-tuple-element.36), channel_id=1, source_target_pairs={{0,28},{4,0},{8,4},{12,8},{16,12},{20,16},{24,20},{28,24},{1,29},{... | collective-permute-start | bytes 147464 | tf_op jit(solution)/shard_map/ppermute | solution.py:23
  126.9 7.9 %collective-permute-start.28 = (bf16[64,384]{1,0:T(8,128)(2,1)S(1)}, bf16[64,384]{1,0:T(8,128)(2,1)S(1)}, u32[]{:S(2)}, u32[]{:S(2)}) collective-permute-start(bf16[64,384]{1,0:T(8,128)(2,1)S(1)} %get-tuple-element.35), channel_id=1, source_target_pairs={{0,4},{4,8},{8,12},{12,16},{16,20},{20,24},{24,28},{28,0},{1,5},{5... | collective-permute-start | bytes 147464 | tf_op jit(solution)/shard_map/ppermute | solution.py:23
  126.9 11.5 %collective-permute-start.27 = (bf16[64,384]{1,0:T(8,128)(2,1)S(1)}, bf16[64,384]{1,0:T(8,128)(2,1)S(1)}, u32[]{:S(2)}, u32[]{:S(2)}) collective-permute-start(bf16[64,384]{1,0:T(8,128)(2,1)S(1)} %get-tuple-element.34), channel_id=1, source_target_pairs={{0,24},{4,28},{8,0},{12,4},{16,8},{20,12},{24,16},{28,20},{1,25},{... | collective-permute-start | bytes 147464 | tf_op jit(solution)/shard_map/ppermute | solution.py:23
  129.8 8.6 %collective-permute-start.26 = (bf16[64,384]{1,0:T(8,128)(2,1)S(1)}, bf16[64,384]{1,0:T(8,128)(2,1)S(1)}, u32[]{:S(2)}, u32[]{:S(2)}) collective-permute-start(bf16[64,384]{1,0:T(8,128)(2,1)S(1)} %get-tuple-element.33), channel_id=1, source_target_pairs={{0,8},{4,12},{8,16},{12,20},{16,24},{20,28},{24,0},{28,4},{1,9},{5... | collective-permute-start | bytes 147464 | tf_op jit(solution)/shard_map/ppermute | solution.py:23
  129.8 8.5 %collective-permute-start.25 = (bf16[64,384]{1,0:T(8,128)(2,1)S(1)}, bf16[64,384]{1,0:T(8,128)(2,1)S(1)}, u32[]{:S(2)}, u32[]{:S(2)}) collective-permute-start(bf16[64,384]{1,0:T(8,128)(2,1)S(1)} %get-tuple-element.32), channel_id=1, source_target_pairs={{0,20},{4,24},{8,28},{12,0},{16,4},{20,8},{24,12},{28,16},{1,21},{... | collective-permute-start | bytes 147464 | tf_op jit(solution)/shard_map/ppermute | solution.py:23
  133.6 8.1 %collective-permute-start.24 = (bf16[64,384]{1,0:T(8,128)(2,1)S(1)}, bf16[64,384]{1,0:T(8,128)(2,1)S(1)}, u32[]{:S(2)}, u32[]{:S(2)}) collective-permute-start(bf16[64,384]{1,0:T(8,128)(2,1)S(1)} %get-tuple-element.31), channel_id=1, source_target_pairs={{0,12},{4,16},{8,20},{12,24},{16,28},{20,0},{24,4},{28,8},{1,13},{... | collective-permute-start | bytes 147464 | tf_op jit(solution)/shard_map/ppermute | solution.py:23
  134.8 8.0 %collective-permute-start.23 = (bf16[64,384]{1,0:T(8,128)(2,1)S(1)}, bf16[64,384]{1,0:T(8,128)(2,1)S(1)}, u32[]{:S(2)}, u32[]{:S(2)}) collective-permute-start(bf16[64,384]{1,0:T(8,128)(2,1)S(1)} %get-tuple-element.30), channel_id=1, source_target_pairs={{0,16},{4,20},{8,24},{12,28},{16,0},{20,4},{24,8},{28,12},{1,17},{... | collective-permute-start | bytes 147464 | tf_op jit(solution)/shard_map/ppermute | solution.py:23
where the time goes:
time: 145 us; the launch traced here: 144 us
  starting transfers between devices  67.6 us (47%)
  waiting for transfers between devices  32 us (22%)
  blocking collectives  25.2 us (17%)
  Pallas kernels  15.3 us (11%)
  matrix products  1.6 us (1%)
  other arithmetic  1.5 us (1%)
    ppermute x28, starting transfers between devices, shifted(): lax.ppermute(value, axis, [(i, (i + steps) % count) for i in range(count)])  53.1 us
    ppermute x28, waiting for transfers between devices, shifted(): lax.ppermute(value, axis, [(i, (i + steps) % count) for i in range(count)])  25.9 us
    all_to_all x1, blocking collectives, exchanged(): return lax.all_to_all(value, axis, split_axis=0, concat_axis=0, tiled=True)  25.2 us
    all_to_all x2, starting transfers between devices, exchanged(): return lax.all_to_all(value, axis, split_axis=0, concat_axis=0, tiled=True)  10.5 us
    pallas_call x2, Pallas kernels, transport(): pl.pallas_call(transport_body, grid=(steps,), in_specs=specs, out_specs=p...  7.24 us
    pallas_call x2, Pallas kernels, gram_tile(): pl.pallas_call(functools.partial(gram_body, apart), in_specs=[pl.BlockSpe...  4.46 us
    ppermute x1, waiting for transfers between devices, on_device(): same = lax.ppermute(jnp.where(even, low, high), PLANE, to_same)  3.64 us
    ppermute x1, starting transfers between devices, on_device(): same = lax.ppermute(jnp.where(even, low, high), PLANE, to_same)  2.93 us
  transfers between devices with their start and end apart: 32, of which 17 were waited for; matrix products, arithmetic and copies ran while one was open for 1% of the time, Pallas kernels for 6%

commit v1 on v0

--- a/solution.py
+++ b/solution.py
@@ -322,9 +322,7 @@
         )
         for c in chosen
     ]
-    weighted = jnp.concatenate([(precision * j).astype(jnp.bfloat16) for j in jac], axis=1)
-    cut = tracers * 5 // 8
-    weighted = [weighted[:, :cut], weighted[:, cut:]]
+    weighted = [(precision * j).astype(jnp.bfloat16) for j in jac]
     low, high = [j.astype(jnp.bfloat16) for j in jac]
 
     pairs = [(i // peers, i % peers) for i in range(group * peers)]
@@ -347,7 +345,7 @@
 
     depth = lax.axis_size("z")
     tile = gram_tile(place, [own, across, *other], cols[0], 0)[0]
-    parts = exchanged(tile.reshape(depth, half // depth, cut), "z")
+    parts = exchanged(tile.reshape(depth, half // depth, half), "z")
     total = jnp.sum(parts.astype(jnp.float32), axis=0)
     blocks = gram_tile(place, [own, across, *other], cols[1], depth)
     last = blocks[0]

time: 145 us -> 145 us (level)
  starting transfers between devices: 67.6 us -> 70.3 us
  waiting for transfers between devices: 32 us -> 30.5 us
    ppermute x28, starting transfers between devices: 53.1 us -> 55.7 us  [shifted(): lax.ppermute(value, axis, [(i, (i + steps) % count) for i in range(count)])]
    ppermute x28, waiting for transfers between devices: 25.9 us -> 24.3 us  [shifted(): lax.ppermute(value, axis, [(i, (i + steps) % count) for i in range(count)])]
  transfers between devices with their start and end apart: 32 -> 32, of which waited for: 17 -> 14; matrix products, arithmetic and copies ran while one was open for 1% -> 1% of each run, Pallas kernels for 6% -> 6%
where the time goes in v1:
time: 145 us; the launch traced here: 144 us
  starting transfers between devices  70.3 us (48%)
  waiting for transfers between devices  30.5 us (21%)
  blocking collectives  25.2 us (17%)
  Pallas kernels  14.9 us (10%)
  matrix products  1.6 us (1%)
  other arithmetic  1.48 us (1%)
    ppermute x28, starting transfers between devices, shifted(): lax.ppermute(value, axis, [(i, (i + steps) % count) for i in range(count)])  55.7 us
    all_to_all x1, blocking collectives, exchanged(): return lax.all_to_all(value, axis, split_axis=0, concat_axis=0, tiled=True)  25.2 us
    ppermute x28, waiting for transfers between devices, shifted(): lax.ppermute(value, axis, [(i, (i + steps) % count) for i in range(count)])  24.3 us
    all_to_all x2, starting transfers between devices, exchanged(): return lax.all_to_all(value, axis, split_axis=0, concat_axis=0, tiled=True)  10.4 us
    pallas_call x2, Pallas kernels, transport(): pl.pallas_call(transport_body, grid=(steps,), in_specs=specs, out_specs=p...  7.24 us
    pallas_call x2, Pallas kernels, gram_tile(): pl.pallas_call(functools.partial(gram_body, apart), in_specs=[pl.BlockSpe...  4.11 us
    ppermute x1, waiting for transfers between devices, on_device(): same = lax.ppermute(jnp.where(even, low, high), PLANE, to_same)  3.74 us
    ppermute x1, starting transfers between devices, on_device(): same = lax.ppermute(jnp.where(even, low, high), PLANE, to_same)  2.93 us
  transfers between devices with their start and end apart: 32, of which 14 were waited for; matrix products, arithmetic and copies ran while one was open for 1% of the time, Pallas kernels for 6%

profile of v1, /device:TPU:4, one launch (start us, length us, event | category | flops | bytes accessed | tf_op | source)
XLA Modules:
  0.0 144.4 jit_solution(18243142891308851800)
XLA Ops:
  0.0 2.5 %edges.1 = (bf16[2320,128]{1,0:T(8,128)(2,1)S(1)}, bf16[2320,128]{1,0:T(8,128)(2,1)S(1)}, bf16[784,128]{1,0:T(8,128)(2,1)}, bf16[784,128]{1,0:T(8,128)(2,1)}) custom-call(f32[4096,128]{1,0:T(8,128)} %bitcast.47, f32[4,128]{1,0:T(4,128)} %wind_x_ref.5, f32[4,128]{1,0:T(4,128)} %wind_y_ref.5), custom_call_target="tpu_custom_call" | custom-call | tf_op jit(solution)/shard_map/edges/pallas_call | solution.py:77
  2.5 2.0 %collective-permute-start.2 = (bf16[2320,128]{1,0:T(8,128)(2,1)S(1)}, bf16[2320,128]{1,0:T(8,128)(2,1)S(1)}, u32[]{:S(2)}, u32[]{:S(2)}) collective-permute-start(bf16[2320,128]{1,0:T(8,128)(2,1)S(1)} %get-tuple-element.23), channel_id=1, source_target_pairs={{0,4},{4,8},{8,12},{12,16},{16,20},{20,24},{24,28},{28,32},{32,36}... | collective-permute-start | bytes 1781768 | tf_op jit(solution)/shard_map/ppermute | solution.py:23
  4.5 7.1 %collective-permute-start.3 = (bf16[2320,128]{1,0:T(8,128)(2,1)S(1)}, bf16[2320,128]{1,0:T(8,128)(2,1)S(1)}, u32[]{:S(2)}, u32[]{:S(2)}) collective-permute-start(bf16[2320,128]{1,0:T(8,128)(2,1)S(1)} %get-tuple-element.24), channel_id=1, source_target_pairs={{0,252},{4,0},{8,4},{12,8},{16,12},{20,16},{24,20},{28,24},{32,28}... | collective-permute-start | bytes 1781768 | tf_op jit(solution)/shard_map/ppermute | solution.py:23
  11.6 0.2 convert_reduce_fusion.2
  11.8 0.1 convert_reduce_fusion.1
  11.9 0.1 fusion.8
  12.1 0.1 iota_compare_fusion
  12.2 1.1 fusion
  13.3 6.9 %all-to-all-start = ((bf16[64,8,256]{2,1,0:T(8,128)(2,1)}), bf16[64,8,256]{2,1,0:T(8,128)(2,1)S(1)}, u32[]{:S(2)}, u32[]{:S(2)}) async-start(bf16[64,8,256]{2,1,0:T(8,128)(2,1)} %fusion), calls=%async_computation | async-start | bytes 524288 | tf_op jit(solution)/shard_map/all_to_all | solution.py:27
  20.2 1.6 %collective-permute-start = (bf16[784,128]{1,0:T(8,128)(2,1)}, bf16[784,128]{1,0:T(8,128)(2,1)S(1)}, u32[]{:S(2)}, u32[]{:S(2)}) collective-permute-start(bf16[784,128]{1,0:T(8,128)(2,1)} %get-tuple-element.21), channel_id=1, source_target_pairs={{0,4},{4,8},{8,12},{12,16},{16,20},{20,24},{24,28},{28,32},{32,36}... | collective-permute-start | bytes 602120 | tf_op jit(solution)/shard_map/ppermute | solution.py:23
  21.9 4.7 %collective-permute-start.1 = (bf16[784,128]{1,0:T(8,128)(2,1)}, bf16[784,128]{1,0:T(8,128)(2,1)S(1)}, u32[]{:S(2)}, u32[]{:S(2)}) collective-permute-start(bf16[784,128]{1,0:T(8,128)(2,1)} %get-tuple-element.22), channel_id=1, source_target_pairs={{0,252},{4,0},{8,4},{12,8},{16,12},{20,16},{24,20},{28,24},{32,28}... | collective-permute-start | bytes 602120 | tf_op jit(solution)/shard_map/ppermute | solution.py:23
  26.5 0.1 stack.71.place_ref
  26.7 0.0 collective-permute-done.2.a0.a1.a2.a_winds
  26.7 2.3 %collective-permute-done.3.b0.b1.b2.b_winds = bf16[2320,128]{1,0:T(8,128)(2,1)S(1)} collective-permute-done((bf16[2320,128]{1,0:T(8,128)(2,1)S(1)}, bf16[2320,128]{1,0:T(8,128)(2,1)S(1)}, u32[]{:S(2)}, u32[]{:S(2)}) %collective-permute-start.3) | collective-permute-done | bytes 593952 | tf_op jit(solution)/shard_map/ppermute | solution.py:23
  28.9 5.0 %transport.2.refs_0_ = bf16[1024,512]{1,0:T(8,128)(2,1)S(1)} custom-call(f32[4096,128]{1,0:T(8,128)} %bitcast.48, bf16[2320,128]{1,0:T(8,128)(2,1)S(1)} %collective-permute-done.2.a0.a1.a2.a_winds, bf16[2320,128]{1,0:T(8,128)(2,1)S(1)} %collective-permute-done.2.a0.a1.a2.a_winds, bf16[2320,128]{1,0:T(8,128)(2,1)S(1)} %collective-permute-done.2.a0.a1.a2.a_winds, ...), custom_call_target="tpu_custom_call" | custom-call | tf_op jit(solution)/shard_map/transport/pallas_call | solution.py:161
  34.0 1.7 %collective-permute-done.a0.a1.a2.a_winds = bf16[784,128]{1,0:T(8,128)(2,1)S(1)} collective-permute-done((bf16[784,128]{1,0:T(8,128)(2,1)}, bf16[784,128]{1,0:T(8,128)(2,1)S(1)}, u32[]{:S(2)}, u32[]{:S(2)}) %collective-permute-start) | collective-permute-done | bytes 200736 | tf_op jit(solution)/shard_map/ppermute | solution.py:23
  35.6 2.2 %transport.3.low_ref.high_ref = bf16[1024,512]{1,0:T(8,128)(2,1)S(1)} custom-call(f32[4096,128]{1,0:T(8,128)} %bitcast.49, bf16[784,128]{1,0:T(8,128)(2,1)S(1)} %collective-permute-done.a0.a1.a2.a_winds, bf16[784,128]{1,0:T(8,128)(2,1)S(1)} %collective-permute-done.a0.a1.a2.a_winds, ...), custom_call_target="tpu_custom_call", output_to_operand_aliasing={{}: (11, {})} | custom-call | tf_op jit(solution)/shard_map/transport/pallas_call | solution.py:161
  37.9 1.1 jacobian.1
  39.0 25.2 %all_to_all.15 = bf16[64,8,512]{2,1,0:T(8,128)(2,1)S(1)} all-to-all(bf16[64,8,512]{2,1,0:T(8,128)(2,1)S(1)} %bitcast.45), channel_id=1, replica_groups=mesh['xl'=2,'y'=4,'z'=8,'xh'=2,'core'=2] {'xl','y','z'}, dimensions={0} | all-to-all | bytes 1048576 | tf_op jit(solution)/shard_map/all_to_all | solution.py:27
  64.3 0.3 fusion.3
  64.5 0.3 broadcast_select_fusion
  64.8 2.9 %collective-permute-start.4 = (bf16[128,512]{1,0:T(8,128)(2,1)S(1)}, bf16[128,512]{1,0:T(8,128)(2,1)S(1)}, u32[]{:S(2)}, u32[]{:S(2)}) collective-permute-start(bf16[128,512]{1,0:T(8,128)(2,1)S(1)} %get-tuple-element.38), channel_id=1, source_target_pairs={{0,0},{1,64},{2,128},{3,192},{32,32},{33,96},{34,160},{35,224},{64... | collective-permute-start | bytes 393224 | tf_op jit(solution)/shard_map/ppermute | solution.py:331
  67.7 1.2 collective-permute-start.5
  68.9 3.7 %collective-permute-done.4 = bf16[128,512]{1,0:T(8,128)(2,1)S(1)} collective-permute-done((bf16[128,512]{1,0:T(8,128)(2,1)S(1)}, bf16[128,512]{1,0:T(8,128)(2,1)S(1)}, u32[]{:S(2)}, u32[]{:S(2)}) %collective-permute-start.4) | collective-permute-done | bytes 131104 | tf_op jit(solution)/shard_map/ppermute | solution.py:331
  72.7 2.4 %collective-permute-done.5 = bf16[128,512]{1,0:T(8,128)(2,1)S(1)} collective-permute-done((bf16[128,512]{1,0:T(8,128)(2,1)S(1)}, bf16[128,512]{1,0:T(8,128)(2,1)S(1)}, u32[]{:S(2)}, u32[]{:S(2)}) %collective-permute-start.5) | collective-permute-done | bytes 131104 | tf_op jit(solution)/shard_map/ppermute | solution.py:332
  75.1 0.1 collective-permute-start.6
  75.2 0.1 multiply_convert_fusion.1
  75.3 3.9 %collective-permute-start.9 = (bf16[128,512]{1,0:T(8,128)(2,1)S(1)}, bf16[128,512]{1,0:T(8,128)(2,1)S(1)}, u32[]{:S(2)}, u32[]{:S(2)}) collective-permute-start(bf16[128,512]{1,0:T(8,128)(2,1)S(1)} %get-tuple-element.43.refs_4_), channel_id=1, source_target_pairs={{0,128},{128,0},{1,129},{129,1},{2,130},{130,2},{3,131},{131,3},{4... | collective-permute-start | bytes 393224 | tf_op jit(solution)/shard_map/ppermute | solution.py:23
  79.2 0.6 collective-permute-start.10
  79.7 1.7 %collective-permute-start.11 = (bf16[128,512]{1,0:T(8,128)(2,1)S(1)}, bf16[128,512]{1,0:T(8,128)(2,1)S(1)}, u32[]{:S(2)}, u32[]{:S(2)}) collective-permute-start(bf16[128,512]{1,0:T(8,128)(2,1)S(1)} %get-tuple-element.43.refs_4_), channel_id=1, source_target_pairs={{0,64},{32,96},{64,0},{96,32},{1,65},{33,97},{65,1},{97,33},{2,66}... | collective-permute-start | bytes 393224 | tf_op jit(solution)/shard_map/ppermute | solution.py:23
  81.4 2.3 %collective-permute-start.12 = (bf16[128,512]{1,0:T(8,128)(2,1)S(1)}, bf16[128,512]{1,0:T(8,128)(2,1)S(1)}, u32[]{:S(2)}, u32[]{:S(2)}) collective-permute-start(bf16[128,512]{1,0:T(8,128)(2,1)S(1)} %get-tuple-element.43.refs_4_), channel_id=1, source_target_pairs={{0,96},{32,0},{64,32},{96,64},{1,97},{33,1},{65,33},{97,65},{2,98}... | collective-permute-start | bytes 393224 | tf_op jit(solution)/shard_map/ppermute | solution.py:23
  83.8 3.7 %collective-permute-done.9.refs_5_ = bf16[128,512]{1,0:T(8,128)(2,1)S(1)} collective-permute-done((bf16[128,512]{1,0:T(8,128)(2,1)S(1)}, bf16[128,512]{1,0:T(8,128)(2,1)S(1)}, u32[]{:S(2)}, u32[]{:S(2)}) %collective-permute-start.9) | collective-permute-done | bytes 131104 | tf_op jit(solution)/shard_map/ppermute | solution.py:23
  87.5 1.6 %collective-permute-start.7 = (bf16[256,512]{1,0:T(8,128)(2,1)S(1)}, bf16[256,512]{1,0:T(8,128)(2,1)S(1)}, u32[]{:S(2)}, u32[]{:S(2)}) collective-permute-start(bf16[256,512]{1,0:T(8,128)(2,1)S(1)} %constant_dynamic-update-slice_fusion.refs_0_), channel_id=1, source_target_pairs={{0,1},{1,0},{2,3},{3,2},{4,5},{5,4},{6,7},{7,6},{8,9},{9,8},{10,11... | collective-permute-start | bytes 786440 | tf_op jit(solution)/shard_map/ppermute | solution.py:23
  89.1 0.0 collective-permute-start.8
  89.1 0.6 collective-permute-start.13
  89.7 0.0 collective-permute-start.14
  89.8 0.1 collective-permute-done.12.refs_8_
  89.8 3.3 %collective-permute-start.15 = (bf16[128,512]{1,0:T(8,128)(2,1)S(1)}, bf16[128,512]{1,0:T(8,128)(2,1)S(1)}, u32[]{:S(2)}, u32[]{:S(2)}) collective-permute-start(bf16[128,512]{1,0:T(8,128)(2,1)S(1)} %collective-permute-done.9.refs_5_), channel_id=1, source_target_pairs={{0,96},{32,0},{64,32},{96,64},{1,97},{33,1},{65,33},{97,65},{2,98}... | collective-permute-start | bytes 393224 | tf_op jit(solution)/shard_map/ppermute | solution.py:23
  93.1 5.9 %collective-permute-done.13.refs_9_ = bf16[128,512]{1,0:T(8,128)(2,1)S(1)} collective-permute-done((bf16[128,512]{1,0:T(8,128)(2,1)S(1)}, bf16[128,512]{1,0:T(8,128)(2,1)S(1)}, u32[]{:S(2)}, u32[]{:S(2)}) %collective-permute-start.13) | collective-permute-done | bytes 131104 | tf_op jit(solution)/shard_map/ppermute | solution.py:23
  99.0 0.6 collective-permute-done.15.refs_11_
  99.6 2.4 %gram.2 = bf16[512,512]{1,0:T(8,128)(2,1)} custom-call(s32[17]{0:T(128)S(1)} %stack.71.place_ref, bf16[256,512]{1,0:T(8,128)(2,1)S(1)} %constant_dynamic-update-slice_fusion.refs_0_, bf16[256,512]{1,0:T(8,128)(2,1)S(1)} %collective-permute-done.6.refs_1_, bf16[256,512]{1,0:T(8,128)(2,1)S(1)} %collective-permute-done.7.refs_2_, ...), custom_call_target="tpu_custom_call" | custom-call | tf_op jit(solution)/shard_map/gram/pallas_call | solution.py:253
  102.1 3.5 %all-to-all-start.2 = ((bf16[8,64,512]{2,1,0:T(8,128)(2,1)}), bf16[8,64,512]{2,1,0:T(8,128)(2,1)S(1)}, u32[]{:S(2)}, u32[]{:S(2)}) async-start(bf16[8,64,512]{2,1,0:T(8,128)(2,1)} %bitcast.28), calls=%async_computation.2 | async-start | bytes 1048576 | tf_op jit(solution)/shard_map/all_to_all | solution.py:27
  105.6 0.1 collective-permute-start.16
  105.7 0.4 collective-permute-start.17
  106.1 3.8 %collective-permute-start.18 = (bf16[128,512]{1,0:T(8,128)(2,1)S(1)}, bf16[128,512]{1,0:T(8,128)(2,1)S(1)}, u32[]{:S(2)}, u32[]{:S(2)}) collective-permute-start(bf16[128,512]{1,0:T(8,128)(2,1)S(1)} %get-tuple-element.44.refs_4_), channel_id=1, source_target_pairs={{0,64},{32,96},{64,0},{96,32},{1,65},{33,97},{65,1},{97,33},{2,66}... | collective-permute-start | bytes 393224 | tf_op jit(solution)/shard_map/ppermute | solution.py:23
  109.9 0.8 collective-permute-done.16.refs_5_
  110.6 1.3 collective-permute-start.20
  111.9 3.3 %collective-permute-start.21 = (bf16[128,512]{1,0:T(8,128)(2,1)S(1)}, bf16[128,512]{1,0:T(8,128)(2,1)S(1)}, u32[]{:S(2)}, u32[]{:S(2)}) collective-permute-start(bf16[128,512]{1,0:T(8,128)(2,1)S(1)} %collective-permute-done.16.refs_5_), channel_id=1, source_target_pairs={{0,64},{32,96},{64,0},{96,32},{1,65},{33,97},{65,1},{97,33},{2,66}... | collective-permute-start | bytes 393224 | tf_op jit(solution)/shard_map/ppermute | solution.py:23
  115.2 1.8 %collective-permute-done.18.refs_7_ = bf16[128,512]{1,0:T(8,128)(2,1)S(1)} collective-permute-done((bf16[128,512]{1,0:T(8,128)(2,1)S(1)}, bf16[128,512]{1,0:T(8,128)(2,1)S(1)}, u32[]{:S(2)}, u32[]{:S(2)}) %collective-permute-start.18) | collective-permute-done | bytes 131104 | tf_op jit(solution)/shard_map/ppermute | solution.py:23
  117.0 2.3 %collective-permute-done.20.refs_9_ = bf16[128,512]{1,0:T(8,128)(2,1)S(1)} collective-permute-done((bf16[128,512]{1,0:T(8,128)(2,1)S(1)}, bf16[128,512]{1,0:T(8,128)(2,1)S(1)}, u32[]{:S(2)}, u32[]{:S(2)}) %collective-permute-start.20) | collective-permute-done | bytes 131104 | tf_op jit(solution)/shard_map/ppermute | solution.py:23
  119.3 2.3 %collective-permute-done.21.refs_10_ = bf16[128,512]{1,0:T(8,128)(2,1)S(1)} collective-permute-done((bf16[128,512]{1,0:T(8,128)(2,1)S(1)}, bf16[128,512]{1,0:T(8,128)(2,1)S(1)}, u32[]{:S(2)}, u32[]{:S(2)}) %collective-permute-start.21) | collective-permute-done | bytes 131104 | tf_op jit(solution)/shard_map/ppermute | solution.py:23
  121.7 1.7 %gram.3 = (f32[64,512]{1,0:T(8,128)S(1)}, bf16[64,512]{1,0:T(8,128)(2,1)S(1)}, bf16[64,512]{1,0:T(8,128)(2,1)S(1)}, bf16[64,512]{1,0:T(8,128)(2,1)S(1)}, bf16[64...) custom-call(s32[17]{0:T(128)S(1)} %stack.71.place_ref, ...), custom_call_target="tpu_custom_call" | custom-call | tf_op jit(solution)/shard_map/gram/pallas_call | solution.py:253
  123.4 5.5 %collective-permute-start.23 = (bf16[64,512]{1,0:T(8,128)(2,1)S(1)}, bf16[64,512]{1,0:T(8,128)(2,1)S(1)}, u32[]{:S(2)}, u32[]{:S(2)}) collective-permute-start(bf16[64,512]{1,0:T(8,128)(2,1)S(1)} %get-tuple-element.30), channel_id=1, source_target_pairs={{0,16},{4,20},{8,24},{12,28},{16,0},{20,4},{24,8},{28,12},{1,17},{... | collective-permute-start | bytes 196616 | tf_op jit(solution)/shard_map/ppermute | solution.py:23
  128.9 0.6 collective-permute-start.24
  129.4 4.4 %collective-permute-start.25 = (bf16[64,512]{1,0:T(8,128)(2,1)S(1)}, bf16[64,512]{1,0:T(8,128)(2,1)S(1)}, u32[]{:S(2)}, u32[]{:S(2)}) collective-permute-start(bf16[64,512]{1,0:T(8,128)(2,1)S(1)} %get-tuple-element.32), channel_id=1, source_target_pairs={{0,20},{4,24},{8,28},{12,0},{16,4},{20,8},{24,12},{28,16},{1,21},{... | collective-permute-start | bytes 196616 | tf_op jit(solution)/shard_map/ppermute | solution.py:23
  133.9 0.6 collective-permute-start.26
  134.5 3.6 %collective-permute-start.27 = (bf16[64,512]{1,0:T(8,128)(2,1)S(1)}, bf16[64,512]{1,0:T(8,128)(2,1)S(1)}, u32[]{:S(2)}, u32[]{:S(2)}) collective-permute-start(bf16[64,512]{1,0:T(8,128)(2,1)S(1)} %get-tuple-element.34), channel_id=1, source_target_pairs={{0,24},{4,28},{8,0},{12,4},{16,8},{20,12},{24,16},{28,20},{1,25},{... | collective-permute-start | bytes 196616 | tf_op jit(solution)/shard_map/ppermute | solution.py:23
  138.0 0.6 collective-permute-start.28
  138.6 0.5 collective-permute-done.24
  139.1 2.2 %collective-permute-start.29 = (bf16[64,512]{1,0:T(8,128)(2,1)S(1)}, bf16[64,512]{1,0:T(8,128)(2,1)S(1)}, u32[]{:S(2)}, u32[]{:S(2)}) collective-permute-start(bf16[64,512]{1,0:T(8,128)(2,1)S(1)} %get-tuple-element.36), channel_id=1, source_target_pairs={{0,28},{4,0},{8,4},{12,8},{16,12},{20,16},{24,20},{28,24},{1,29},{... | collective-permute-start | bytes 196616 | tf_op jit(solution)/shard_map/ppermute | solution.py:23
  141.3 2.2 %collective-permute-done.28 = bf16[64,512]{1,0:T(8,128)(2,1)S(1)} collective-permute-done((bf16[64,512]{1,0:T(8,128)(2,1)S(1)}, bf16[64,512]{1,0:T(8,128)(2,1)S(1)}, u32[]{:S(2)}, u32[]{:S(2)}) %collective-permute-start.28) | collective-permute-done | bytes 65568 | tf_op jit(solution)/shard_map/ppermute | solution.py:23
  143.5 0.1 convert_add_fusion
  143.6 0.1 convert_reduce_fusion
  143.7 0.7 pad_maximum_fusion
  (34 shorter events, 0.1 us)
Async XLA Ops:
  0.0 11.6 %copy-start.3 = (s32[128,1]{0,1:T(1,128)S(1)}, s32[128,1]{0,1:T(1,128)}, u32[]{:S(2)}) copy-start(s32[128,1]{0,1:T(1,128)} %param.9) | copy-start | bytes 1540
  0.0 11.8 %copy-start.2 = (bf16[128,512]{1,0:T(8,128)(2,1)S(1)}, bf16[128,512]{1,0:T(8,128)(2,1)}, u32[]{:S(2)}) copy-start(bf16[128,512]{1,0:T(8,128)(2,1)} %param.10) | copy-start | bytes 393220
  0.0 26.6 %copy-start.4 = (bf16[128]{0:T(256)(128)(2,1)S(1)}, bf16[128]{0:T(256)(128)(2,1)}, u32[]{:S(2)}) copy-start(bf16[128]{0:T(256)(128)(2,1)} %param.11) | copy-start | bytes 772
  0.0 28.9 %copy-start = (f32[4,128]{1,0:T(4,128)S(1)}, f32[4,128]{1,0:T(4,128)}, u32[]{:S(2)}) copy-start(f32[4,128]{1,0:T(4,128)} %wind_x_ref.5) | copy-start | bytes 6148
  0.0 28.9 %copy-start.1 = (f32[4,128]{1,0:T(4,128)S(1)}, f32[4,128]{1,0:T(4,128)}, u32[]{:S(2)}) copy-start(f32[4,128]{1,0:T(4,128)} %wind_y_ref.5) | copy-start | bytes 6148
  2.5 24.1 %collective-permute-start.2 = (bf16[2320,128]{1,0:T(8,128)(2,1)S(1)}, bf16[2320,128]{1,0:T(8,128)(2,1)S(1)}, u32[]{:S(2)}, u32[]{:S(2)}) collective-permute-start(bf16[2320,128]{1,0:T(8,128)(2,1)S(1)} %get-tuple-element.23), channel_id=1, source_target_pairs={{0,4},{4,8},{8,12},{12,16},{16,20},{20,24},{24,28},{28,32},{32,36}... | collective-permute-start | bytes 1781768 | tf_op jit(solution)/shard_map/ppermute | solution.py:23
  4.5 24.4 %collective-permute-start.3 = (bf16[2320,128]{1,0:T(8,128)(2,1)S(1)}, bf16[2320,128]{1,0:T(8,128)(2,1)S(1)}, u32[]{:S(2)}, u32[]{:S(2)}) collective-permute-start(bf16[2320,128]{1,0:T(8,128)(2,1)S(1)} %get-tuple-element.24), channel_id=1, source_target_pairs={{0,252},{4,0},{8,4},{12,8},{16,12},{20,16},{24,20},{28,24},{32,28}... | collective-permute-start | bytes 1781768 | tf_op jit(solution)/shard_map/ppermute | solution.py:23
  13.3 24.6 %all-to-all-start = ((bf16[64,8,256]{2,1,0:T(8,128)(2,1)}), bf16[64,8,256]{2,1,0:T(8,128)(2,1)S(1)}, u32[]{:S(2)}, u32[]{:S(2)}) async-start(bf16[64,8,256]{2,1,0:T(8,128)(2,1)} %fusion), calls=%async_computation | async-start | bytes 524288 | tf_op jit(solution)/shard_map/all_to_all | solution.py:27
  20.2 15.4 %collective-permute-start = (bf16[784,128]{1,0:T(8,128)(2,1)}, bf16[784,128]{1,0:T(8,128)(2,1)S(1)}, u32[]{:S(2)}, u32[]{:S(2)}) collective-permute-start(bf16[784,128]{1,0:T(8,128)(2,1)} %get-tuple-element.21), channel_id=1, source_target_pairs={{0,4},{4,8},{8,12},{12,16},{16,20},{20,24},{24,28},{28,32},{32,36}... | collective-permute-start | bytes 602120 | tf_op jit(solution)/shard_map/ppermute | solution.py:23
  21.9 13.8 %collective-permute-start.1 = (bf16[784,128]{1,0:T(8,128)(2,1)}, bf16[784,128]{1,0:T(8,128)(2,1)S(1)}, u32[]{:S(2)}, u32[]{:S(2)}) collective-permute-start(bf16[784,128]{1,0:T(8,128)(2,1)} %get-tuple-element.22), channel_id=1, source_target_pairs={{0,252},{4,0},{8,4},{12,8},{16,12},{20,16},{24,20},{28,24},{32,28}... | collective-permute-start | bytes 602120 | tf_op jit(solution)/shard_map/ppermute | solution.py:23
  64.8 7.8 %collective-permute-start.4 = (bf16[128,512]{1,0:T(8,128)(2,1)S(1)}, bf16[128,512]{1,0:T(8,128)(2,1)S(1)}, u32[]{:S(2)}, u32[]{:S(2)}) collective-permute-start(bf16[128,512]{1,0:T(8,128)(2,1)S(1)} %get-tuple-element.38), channel_id=1, source_target_pairs={{0,0},{1,64},{2,128},{3,192},{32,32},{33,96},{34,160},{35,224},{64... | collective-permute-start | bytes 393224 | tf_op jit(solution)/shard_map/ppermute | solution.py:331
  67.7 7.4 %collective-permute-start.5 = (bf16[128,512]{1,0:T(8,128)(2,1)S(1)}, bf16[128,512]{1,0:T(8,128)(2,1)S(1)}, u32[]{:S(2)}, u32[]{:S(2)}) collective-permute-start(bf16[128,512]{1,0:T(8,128)(2,1)S(1)} %get-tuple-element.37), channel_id=1, source_target_pairs={{0,32},{1,96},{2,160},{3,224},{32,0},{33,64},{34,128},{35,192},{64... | collective-permute-start | bytes 393224 | tf_op jit(solution)/shard_map/ppermute | solution.py:332
  75.1 14.0 %collective-permute-start.6 = (bf16[256,512]{1,0:T(8,128)(2,1)S(1)}, bf16[256,512]{1,0:T(8,128)(2,1)S(1)}, u32[]{:S(2)}, u32[]{:S(2)}) collective-permute-start(bf16[256,512]{1,0:T(8,128)(2,1)S(1)} %constant_dynamic-update-slice_fusion.refs_0_), channel_id=1, source_target_pairs={{0,2},{2,0},{1,3},{3,1},{4,6},{6,4},{5,7},{7,5},{8,10},{10,8},{9,1... | collective-permute-start | bytes 786440 | tf_op jit(solution)/shard_map/ppermute | solution.py:23
  75.3 12.2 %collective-permute-start.9 = (bf16[128,512]{1,0:T(8,128)(2,1)S(1)}, bf16[128,512]{1,0:T(8,128)(2,1)S(1)}, u32[]{:S(2)}, u32[]{:S(2)}) collective-permute-start(bf16[128,512]{1,0:T(8,128)(2,1)S(1)} %get-tuple-element.43.refs_4_), channel_id=1, source_target_pairs={{0,128},{128,0},{1,129},{129,1},{2,130},{130,2},{3,131},{131,3},{4... | collective-permute-start | bytes 393224 | tf_op jit(solution)/shard_map/ppermute | solution.py:23
  79.2 9.9 %collective-permute-start.10 = (bf16[128,512]{1,0:T(8,128)(2,1)S(1)}, bf16[128,512]{1,0:T(8,128)(2,1)S(1)}, u32[]{:S(2)}, u32[]{:S(2)}) collective-permute-start(bf16[128,512]{1,0:T(8,128)(2,1)S(1)} %get-tuple-element.43.refs_4_), channel_id=1, source_target_pairs={{0,32},{32,64},{64,96},{96,0},{1,33},{33,65},{65,97},{97,1},{2,34}... | collective-permute-start | bytes 393224 | tf_op jit(solution)/shard_map/ppermute | solution.py:23
  79.7 10.0 %collective-permute-start.11 = (bf16[128,512]{1,0:T(8,128)(2,1)S(1)}, bf16[128,512]{1,0:T(8,128)(2,1)S(1)}, u32[]{:S(2)}, u32[]{:S(2)}) collective-permute-start(bf16[128,512]{1,0:T(8,128)(2,1)S(1)} %get-tuple-element.43.refs_4_), channel_id=1, source_target_pairs={{0,64},{32,96},{64,0},{96,32},{1,65},{33,97},{65,1},{97,33},{2,66}... | collective-permute-start | bytes 393224 | tf_op jit(solution)/shard_map/ppermute | solution.py:23
  81.4 8.4 %collective-permute-start.12 = (bf16[128,512]{1,0:T(8,128)(2,1)S(1)}, bf16[128,512]{1,0:T(8,128)(2,1)S(1)}, u32[]{:S(2)}, u32[]{:S(2)}) collective-permute-start(bf16[128,512]{1,0:T(8,128)(2,1)S(1)} %get-tuple-element.43.refs_4_), channel_id=1, source_target_pairs={{0,96},{32,0},{64,32},{96,64},{1,97},{33,1},{65,33},{97,65},{2,98}... | collective-permute-start | bytes 393224 | tf_op jit(solution)/shard_map/ppermute | solution.py:23
  87.5 12.1 %collective-permute-start.7 = (bf16[256,512]{1,0:T(8,128)(2,1)S(1)}, bf16[256,512]{1,0:T(8,128)(2,1)S(1)}, u32[]{:S(2)}, u32[]{:S(2)}) collective-permute-start(bf16[256,512]{1,0:T(8,128)(2,1)S(1)} %constant_dynamic-update-slice_fusion.refs_0_), channel_id=1, source_target_pairs={{0,1},{1,0},{2,3},{3,2},{4,5},{5,4},{6,7},{7,6},{8,9},{9,8},{10,11... | collective-permute-start | bytes 786440 | tf_op jit(solution)/shard_map/ppermute | solution.py:23
  89.1 10.5 %collective-permute-start.8 = (bf16[256,512]{1,0:T(8,128)(2,1)S(1)}, bf16[256,512]{1,0:T(8,128)(2,1)S(1)}, u32[]{:S(2)}, u32[]{:S(2)}) collective-permute-start(bf16[256,512]{1,0:T(8,128)(2,1)S(1)} %collective-permute-done.6.refs_1_), channel_id=1, source_target_pairs={{0,1},{1,0},{2,3},{3,2},{4,5},{5,4},{6,7},{7,6},{8,9},{9,8},{10,11... | collective-permute-start | bytes 786440 | tf_op jit(solution)/shard_map/ppermute | solution.py:23
  89.1 9.9 %collective-permute-start.13 = (bf16[128,512]{1,0:T(8,128)(2,1)S(1)}, bf16[128,512]{1,0:T(8,128)(2,1)S(1)}, u32[]{:S(2)}, u32[]{:S(2)}) collective-permute-start(bf16[128,512]{1,0:T(8,128)(2,1)S(1)} %collective-permute-done.9.refs_5_), channel_id=1, source_target_pairs={{0,32},{32,64},{64,96},{96,0},{1,33},{33,65},{65,97},{97,1},{2,34}... | collective-permute-start | bytes 393224 | tf_op jit(solution)/shard_map/ppermute | solution.py:23
  89.7 9.3 %collective-permute-start.14 = (bf16[128,512]{1,0:T(8,128)(2,1)S(1)}, bf16[128,512]{1,0:T(8,128)(2,1)S(1)}, u32[]{:S(2)}, u32[]{:S(2)}) collective-permute-start(bf16[128,512]{1,0:T(8,128)(2,1)S(1)} %collective-permute-done.9.refs_5_), channel_id=1, source_target_pairs={{0,64},{32,96},{64,0},{96,32},{1,65},{33,97},{65,1},{97,33},{2,66}... | collective-permute-start | bytes 393224 | tf_op jit(solution)/shard_map/ppermute | solution.py:23
  89.8 9.8 %collective-permute-start.15 = (bf16[128,512]{1,0:T(8,128)(2,1)S(1)}, bf16[128,512]{1,0:T(8,128)(2,1)S(1)}, u32[]{:S(2)}, u32[]{:S(2)}) collective-permute-start(bf16[128,512]{1,0:T(8,128)(2,1)S(1)} %collective-permute-done.9.refs_5_), channel_id=1, source_target_pairs={{0,96},{32,0},{64,32},{96,64},{1,97},{33,1},{65,33},{97,65},{2,98}... | collective-permute-start | bytes 393224 | tf_op jit(solution)/shard_map/ppermute | solution.py:23
  102.1 41.5 %all-to-all-start.2 = ((bf16[8,64,512]{2,1,0:T(8,128)(2,1)}), bf16[8,64,512]{2,1,0:T(8,128)(2,1)S(1)}, u32[]{:S(2)}, u32[]{:S(2)}) async-start(bf16[8,64,512]{2,1,0:T(8,128)(2,1)} %bitcast.28), calls=%async_computation.2 | async-start | bytes 1048576 | tf_op jit(solution)/shard_map/all_to_all | solution.py:27
  105.6 5.1 %collective-permute-start.16 = (bf16[128,512]{1,0:T(8,128)(2,1)S(1)}, bf16[128,512]{1,0:T(8,128)(2,1)S(1)}, u32[]{:S(2)}, u32[]{:S(2)}) collective-permute-start(bf16[128,512]{1,0:T(8,128)(2,1)S(1)} %get-tuple-element.44.refs_4_), channel_id=1, source_target_pairs={{0,128},{128,0},{1,129},{129,1},{2,130},{130,2},{3,131},{131,3},{4... | collective-permute-start | bytes 393224 | tf_op jit(solution)/shard_map/ppermute | solution.py:23
  105.7 9.5 %collective-permute-start.17 = (bf16[128,512]{1,0:T(8,128)(2,1)S(1)}, bf16[128,512]{1,0:T(8,128)(2,1)S(1)}, u32[]{:S(2)}, u32[]{:S(2)}) collective-permute-start(bf16[128,512]{1,0:T(8,128)(2,1)S(1)} %get-tuple-element.44.refs_4_), channel_id=1, source_target_pairs={{0,32},{32,64},{64,96},{96,0},{1,33},{33,65},{65,97},{97,1},{2,34}... | collective-permute-start | bytes 393224 | tf_op jit(solution)/shard_map/ppermute | solution.py:23
  106.1 10.9 %collective-permute-start.18 = (bf16[128,512]{1,0:T(8,128)(2,1)S(1)}, bf16[128,512]{1,0:T(8,128)(2,1)S(1)}, u32[]{:S(2)}, u32[]{:S(2)}) collective-permute-start(bf16[128,512]{1,0:T(8,128)(2,1)S(1)} %get-tuple-element.44.refs_4_), channel_id=1, source_target_pairs={{0,64},{32,96},{64,0},{96,32},{1,65},{33,97},{65,1},{97,33},{2,66}... | collective-permute-start | bytes 393224 | tf_op jit(solution)/shard_map/ppermute | solution.py:23
  109.8 7.2 %collective-permute-start.19 = (bf16[128,512]{1,0:T(8,128)(2,1)S(1)}, bf16[128,512]{1,0:T(8,128)(2,1)S(1)}, u32[]{:S(2)}, u32[]{:S(2)}) collective-permute-start(bf16[128,512]{1,0:T(8,128)(2,1)S(1)} %get-tuple-element.44.refs_4_), channel_id=1, source_target_pairs={{0,96},{32,0},{64,32},{96,64},{1,97},{33,1},{65,33},{97,65},{2,98}... | collective-permute-start | bytes 393224 | tf_op jit(solution)/shard_map/ppermute | solution.py:23
  110.6 8.7 %collective-permute-start.20 = (bf16[128,512]{1,0:T(8,128)(2,1)S(1)}, bf16[128,512]{1,0:T(8,128)(2,1)S(1)}, u32[]{:S(2)}, u32[]{:S(2)}) collective-permute-start(bf16[128,512]{1,0:T(8,128)(2,1)S(1)} %collective-permute-done.16.refs_5_), channel_id=1, source_target_pairs={{0,32},{32,64},{64,96},{96,0},{1,33},{33,65},{65,97},{97,1},{2,34}... | collective-permute-start | bytes 393224 | tf_op jit(solution)/shard_map/ppermute | solution.py:23
  111.9 9.8 %collective-permute-start.21 = (bf16[128,512]{1,0:T(8,128)(2,1)S(1)}, bf16[128,512]{1,0:T(8,128)(2,1)S(1)}, u32[]{:S(2)}, u32[]{:S(2)}) collective-permute-start(bf16[128,512]{1,0:T(8,128)(2,1)S(1)} %collective-permute-done.16.refs_5_), channel_id=1, source_target_pairs={{0,64},{32,96},{64,0},{96,32},{1,65},{33,97},{65,1},{97,33},{2,66}... | collective-permute-start | bytes 393224 | tf_op jit(solution)/shard_map/ppermute | solution.py:23
  115.2 6.5 %collective-permute-start.22 = (bf16[128,512]{1,0:T(8,128)(2,1)S(1)}, bf16[128,512]{1,0:T(8,128)(2,1)S(1)}, u32[]{:S(2)}, u32[]{:S(2)}) collective-permute-start(bf16[128,512]{1,0:T(8,128)(2,1)S(1)} %collective-permute-done.16.refs_5_), channel_id=1, source_target_pairs={{0,96},{32,0},{64,32},{96,64},{1,97},{33,1},{65,33},{97,65},{2,98}... | collective-permute-start | bytes 393224 | tf_op jit(solution)/shard_map/ppermute | solution.py:23
  123.4 14.7 %collective-permute-start.23 = (bf16[64,512]{1,0:T(8,128)(2,1)S(1)}, bf16[64,512]{1,0:T(8,128)(2,1)S(1)}, u32[]{:S(2)}, u32[]{:S(2)}) collective-permute-start(bf16[64,512]{1,0:T(8,128)(2,1)S(1)} %get-tuple-element.30), channel_id=1, source_target_pairs={{0,16},{4,20},{8,24},{12,28},{16,0},{20,4},{24,8},{28,12},{1,17},{... | collective-permute-start | bytes 196616 | tf_op jit(solution)/shard_map/ppermute | solution.py:23
  128.9 10.3 %collective-permute-start.24 = (bf16[64,512]{1,0:T(8,128)(2,1)S(1)}, bf16[64,512]{1,0:T(8,128)(2,1)S(1)}, u32[]{:S(2)}, u32[]{:S(2)}) collective-permute-start(bf16[64,512]{1,0:T(8,128)(2,1)S(1)} %get-tuple-element.31), channel_id=1, source_target_pairs={{0,12},{4,16},{8,20},{12,24},{16,28},{20,0},{24,4},{28,8},{1,13},{... | collective-permute-start | bytes 196616 | tf_op jit(solution)/shard_map/ppermute | solution.py:23
  129.4 11.8 %collective-permute-start.25 = (bf16[64,512]{1,0:T(8,128)(2,1)S(1)}, bf16[64,512]{1,0:T(8,128)(2,1)S(1)}, u32[]{:S(2)}, u32[]{:S(2)}) collective-permute-start(bf16[64,512]{1,0:T(8,128)(2,1)S(1)} %get-tuple-element.32), channel_id=1, source_target_pairs={{0,20},{4,24},{8,28},{12,0},{16,4},{20,8},{24,12},{28,16},{1,21},{... | collective-permute-start | bytes 196616 | tf_op jit(solution)/shard_map/ppermute | solution.py:23
  133.9 7.4 %collective-permute-start.26 = (bf16[64,512]{1,0:T(8,128)(2,1)S(1)}, bf16[64,512]{1,0:T(8,128)(2,1)S(1)}, u32[]{:S(2)}, u32[]{:S(2)}) collective-permute-start(bf16[64,512]{1,0:T(8,128)(2,1)S(1)} %get-tuple-element.33), channel_id=1, source_target_pairs={{0,8},{4,12},{8,16},{12,20},{16,24},{20,28},{24,0},{28,4},{1,9},{5... | collective-permute-start | bytes 196616 | tf_op jit(solution)/shard_map/ppermute | solution.py:23
  134.5 6.8 %collective-permute-start.27 = (bf16[64,512]{1,0:T(8,128)(2,1)S(1)}, bf16[64,512]{1,0:T(8,128)(2,1)S(1)}, u32[]{:S(2)}, u32[]{:S(2)}) collective-permute-start(bf16[64,512]{1,0:T(8,128)(2,1)S(1)} %get-tuple-element.34), channel_id=1, source_target_pairs={{0,24},{4,28},{8,0},{12,4},{16,8},{20,12},{24,16},{28,20},{1,25},{... | collective-permute-start | bytes 196616 | tf_op jit(solution)/shard_map/ppermute | solution.py:23
  138.0 5.5 %collective-permute-start.28 = (bf16[64,512]{1,0:T(8,128)(2,1)S(1)}, bf16[64,512]{1,0:T(8,128)(2,1)S(1)}, u32[]{:S(2)}, u32[]{:S(2)}) collective-permute-start(bf16[64,512]{1,0:T(8,128)(2,1)S(1)} %get-tuple-element.35), channel_id=1, source_target_pairs={{0,4},{4,8},{8,12},{12,16},{16,20},{20,24},{24,28},{28,0},{1,5},{5... | collective-permute-start | bytes 196616 | tf_op jit(solution)/shard_map/ppermute | solution.py:23
  139.1 4.4 %collective-permute-start.29 = (bf16[64,512]{1,0:T(8,128)(2,1)S(1)}, bf16[64,512]{1,0:T(8,128)(2,1)S(1)}, u32[]{:S(2)}, u32[]{:S(2)}) collective-permute-start(bf16[64,512]{1,0:T(8,128)(2,1)S(1)} %get-tuple-element.36), channel_id=1, source_target_pairs={{0,28},{4,0},{8,4},{12,8},{16,12},{20,16},{24,20},{28,24},{1,29},{... | collective-permute-start | bytes 196616 | tf_op jit(solution)/shard_map/ppermute | solution.py:23
